TPU v7x, 128 devices: a whole 4x4x4 slice. The times are simulated.
128 devices in a mesh: role: 2 (over x_hi), shard: 16 (over z, y), rep: 4 (over x_lo, core).
Axes of the slice: x: 4 (x_hi: 2, x_lo: 2; x = x_hi * 2 + x_lo), y: 4, z: 4, core: 2. Of those that a mesh axis runs over, the one named last changes fastest.
Arguments:
- qkv_versions: bfloat16 [2, 5120, 7168], P('role', 'rep', 'shard'), may hold values from -0.078125 to 0.078125
- qkv_bias: bfloat16 [2, 7168], P('role'), may hold values from -3 to 3
- o_versions: bfloat16 [2, 5120, 5120], P('role', 'rep', 'shard'), may hold values from -0.078125 to 0.078125
- norm_gain: bfloat16 [2, 5120], P('role'), may hold values from 0.5 to 1.5
- hidden: bfloat16 [2, 1024, 4, 5120], P('role', ('shard', 'rep')), may hold values from -6 to 6
- cache_keys: bfloat16 [2, 1024, 128, 1024], P('role', ('shard', 'rep')), may hold values from -220 to 220
- cache_values: bfloat16 [2, 1024, 128, 1024], P('role', ('shard', 'rep')), may hold values from -6 to 6
- lengths: int32 [2, 1024], P('role', ('shard', 'rep')), may hold values from 2 to 128, as said below
Outputs:
- layer_out: bfloat16 [2, 1024, 4, 5120], P('role', ('shard', 'rep'))
- new_qkv: bfloat16 [2, 5120, 7168], P('role', 'rep', 'shard')
- new_o: bfloat16 [2, 5120, 5120], P('role', 'rep', 'shard')
Inputs may be any that keep to these rules, and one draw needn't show every extreme that they name: `lengths`: in every aligned group of 16 rows of a role at least one row has all 128 positions live.
All inputs are finite; a program needn't handle non-finite values.
Results may differ from a plain program's by a relative error of at most 0.0065.
The roundings to bfloat16 on the way count: a program that leaves them out, or rounds other values in their place, can miss the bound.
Values may be sent and summed in bfloat16 or wider, within the bound.
No kernel may reach another device: no remote copies, remote signals or barrier semaphores. Data moves between devices by JAX's collectives and lax.ppermute only.
A program may use at most 128 MiB of HBM per device.

v0:
```python
import functools
import math

import jax
import jax.numpy as jnp
from jax import lax
from jax.experimental import pallas as pl
from jax.experimental.pallas import tpu as pltpu
from jax.sharding import PartitionSpec as P


FACTOR_A = 40
FACTOR_B = 128
D = 5120
HEADS = 40
KV_HEADS = 8
HEAD_DIM = 128
QDIM = 5120
KVD = 1024
STEPS = 4


EPSILON = 1e-06
ROPE_BASE = 1000000.0


LINES = 4


def shifted(value, axis, steps):
    count = lax.axis_size(axis)
    initial, last = (max(0, -steps), min(count, count - steps))
    return lax.ppermute(value, axis, [(source, source + steps) for source in range(initial, last)])


def along_z(value, steps):
    count = lax.axis_size("shard")
    pairs = [(s, (s + steps * LINES) % count) for s in range(count)]
    return lax.ppermute(value, "shard", pairs)


def mirror_y(value):
    count = lax.axis_size("shard")
    return lax.ppermute(value, "shard", [(s, s ^ 3) for s in range(count)])


def next_y(value):
    count = lax.axis_size("shard")
    return lax.ppermute(value, "shard", [(s, s ^ 1) for s in range(count)])


def other_chip(value):
    return lax.ppermute(value, "rep", [(r, r ^ 2) for r in range(4)])


def other_core(value):
    return lax.ppermute(value, "rep", [(r, r ^ 1) for r in range(4)])


def crossed(even_value, odd_value, even_pair, odd_pair):
    value = jnp.where(lax.axis_index("rep") % 2 == 0, even_value, odd_value)
    reps = lax.axis_size("rep")
    pairs = []
    for s in range(lax.axis_size("shard")):
        for r in range(reps):
            to_shard, to_rep = (even_pair if r % 2 == 0 else odd_pair)(s, r)
            pairs.append((s * reps + r, to_shard * reps + to_rep))
    return lax.ppermute(value, ("shard", "rep"), pairs)


def gather_rows(own):
    count = lax.axis_size("shard")
    below = along_z(own, 1)
    above = along_z(own, -1)
    mirror = mirror_y(own)
    far = crossed(
        below,
        above,
        lambda s, r: ((s + LINES) % count, r),
        lambda s, r: ((s - LINES) % count, r),
    )
    mirror, _ = lax.optimization_barrier((mirror, far))
    mirror_below = along_z(mirror, 1)
    mirror_above = along_z(mirror, -1)
    mirror_far = mirror_y(far)
    return ((own, below, above, far), (mirror, mirror_below, mirror_above, mirror_far))


def gather_weights(own, gate=None, late=None):
    across = other_chip(own)
    pair = next_y(own)
    if gate is not None:
        across, pair, _ = lax.optimization_barrier((across, pair, gate))
    beside = other_core(own)
    pair_beside = other_core(pair)
    across_beside = other_core(across)
    pair_across = crossed(
        pair, across, lambda s, r: (s, r ^ 2), lambda s, r: (s ^ 1, r)
    )
    crossing = pair_across
    if late is not None:
        pair_across = after(pair_across, late)
    pair_across_beside = other_core(pair_across)
    return (
        (own, beside, across, across_beside),
        (pair, pair_beside, pair_across, pair_across_beside),
        crossing,
    )


def after(value, *others):
    return lax.optimization_barrier((value,) + others)[0]


def slot_columns(rows, rep_index):
    width = rows.shape[1] // 4
    return jnp.concatenate(
        [lax.dynamic_slice_in_dim(rows, (rep_index ^ j) * width, width, 1) for j in range(4)], axis=1
    )


def owner_order(shard_index):
    line_z = shard_index // LINES
    high = (shard_index // 2) % 2
    steps = jnp.array([0, -1, 1, 2], jnp.int32)
    owners = jnp.mod(line_z + steps, 4) * 2
    low_first = (1 - shard_index % 2).reshape(1)
    return owners + high, owners + 1 - high, low_first.astype(jnp.int32)


def to_owners(ordered):
    lines = lax.axis_size("shard") // LINES
    groups = [
        [z * LINES + y for z in range(lines) for y in (0, 3)],
        [z * LINES + y for z in range(lines) for y in (1, 2)],
    ]
    return lax.all_to_all(
        ordered, "shard", split_axis=0, concat_axis=0, axis_index_groups=groups, tiled=True
    )


def hadamard_pair():
    modulus = FACTOR_A // 2 - 1
    residues = jnp.arange(modulus, dtype=jnp.int32)
    squares = jnp.arange(1, modulus, dtype=jnp.int32) ** 2 % modulus
    differ = (residues[None, :] - residues[:, None]) % modulus
    residue_mask = jnp.any(differ[:, :, None] == squares[None, None, :], axis=2)
    jacobs = jnp.where(differ == 0, 0.0, jnp.where(residue_mask, 1.0, -1.0)).astype(jnp.float32)
    top_row = jnp.concatenate(
        [jnp.zeros((1, 1), jnp.float32), jnp.ones((1, modulus), jnp.float32)], axis=1
    )
    lower_rows = jnp.concatenate([-jnp.ones((modulus, 1), jnp.float32), jacobs], axis=1)
    paley_core = jnp.eye(modulus + 1, dtype=jnp.float32) + jnp.concatenate(
        [top_row, lower_rows], axis=0
    )
    doubler = jnp.array([[1.0, 1.0], [1.0, -1.0]], jnp.float32)
    outer_factor = jnp.kron(doubler, paley_core)
    indices = jnp.arange(FACTOR_B, dtype=jnp.int32)
    common_bits = indices[:, None] & indices[None, :]
    parity = jnp.zeros((FACTOR_B, FACTOR_B), jnp.int32)
    for bit_level in range(FACTOR_B.bit_length() - 1):
        parity = parity + (common_bits >> bit_level & 1)
    inner_factor = (1 - 2 * (parity % 2)).astype(jnp.float32)
    return (outer_factor, inner_factor)


def fold_kernel(outer_ref, inner_ref, *refs):
    slot_refs, out_ref = refs[:4], refs[4]
    parts = out_ref.shape[1] // FACTOR_B
    sign = (outer_ref[0, 0] * outer_ref[2 * parts, 0]).astype(jnp.bfloat16)
    inner = inner_ref[...]
    stacked = jnp.concatenate([inner, inner * sign], axis=0)
    height = 32

    @pl.loop(0, out_ref.shape[0] // height)
    def _(step):
        span = pl.ds(pl.multiple_of(step * height, height), height)
        totals = [jnp.zeros((height, FACTOR_B), jnp.float32) for _ in range(parts)]
        for slot in range(2):
            for i in range(parts):
                lanes = slice(i * FACTOR_B, (i + 1) * FACTOR_B)
                both = jnp.concatenate(
                    [slot_refs[slot][span, lanes], slot_refs[slot + 2][span, lanes]], axis=1
                )
                mixed = jnp.dot(both, stacked, preferred_element_type=jnp.float32)
                for x in range(parts):
                    totals[x] = totals[x] + outer_ref[slot * parts + i, x] * mixed
        for x in range(parts):
            out_ref[span, x * FACTOR_B : (x + 1) * FACTOR_B] = (
                totals[x] * (1.0 / math.sqrt(D))
            ).astype(jnp.bfloat16)


def rotate_column_part(slots, part_index, part_total):
    outer_factor, inner_factor = hadamard_pair()
    height, width = slots[0].shape
    part_width = FACTOR_A // part_total
    outer_part = lax.dynamic_slice_in_dim(outer_factor, part_index * part_width, part_width, 1)
    outer_part = jnp.concatenate(
        [
            lax.dynamic_slice_in_dim(outer_part, (part_index ^ j) * part_width, part_width, 0)
            for j in range(part_total)
        ],
        axis=0,
    )
    rows = 64
    block = pl.BlockSpec((rows, width), lambda i: (i, 0))
    return pl.pallas_call(
        fold_kernel,
        out_shape=jax.ShapeDtypeStruct((height, width), jnp.bfloat16),
        grid=(height // rows,),
        in_specs=[
            pl.BlockSpec(memory_space=pltpu.SMEM),
            pl.BlockSpec((FACTOR_B, FACTOR_B), lambda i: (0, 0)),
        ]
        + [block] * 4,
        out_specs=block,
        cost_estimate=pl.CostEstimate(flops=4_000_000_000, bytes_accessed=6_000_000, transcendentals=0),
        name="fold_part",
    )(outer_part, inner_factor.astype(jnp.bfloat16), *slots)


def rotate_columns(matrix):
    outer_factor, inner_factor = hadamard_pair()
    height = matrix.shape[0]
    blocks = matrix.reshape(height, FACTOR_A, FACTOR_B)
    inner_mixed = jnp.einsum(
        "mab,by->may", blocks, inner_factor.astype(jnp.bfloat16), preferred_element_type=jnp.float32
    )
    turned = jnp.einsum("may,ax->mxy", inner_mixed, outer_factor, precision=lax.Precision.HIGHEST)
    return (turned.reshape(height, D) * (1.0 / math.sqrt(D))).astype(jnp.bfloat16)


def normalize(states, gain):
    mean_square = jnp.mean(states * states, axis=-1, keepdims=True)
    return (states * lax.rsqrt(mean_square + EPSILON) * gain.astype(jnp.float32)).astype(
        jnp.bfloat16
    )


def spun(vectors, cosine, sine):
    return vectors * cosine + pltpu.roll(vectors, HEAD_DIM // 2, 1) * sine


def attention_kernel(
    part_ref, length_ref, packed_ref, cosine_ref, sine_ref, keys_ref, values_ref, out_ref, spun_ref, sum_ref
):
    block = pl.program_id(0)
    group = part_ref[0] ^ pl.program_id(1)
    cached = keys_ref.shape[1]
    rows = keys_ref.shape[0]
    tokens = rows * STEPS
    piece_heads = packed_ref.shape[2] // HEAD_DIM
    ratio = HEADS // KV_HEADS
    cosine = cosine_ref[...]
    sine = sine_ref[...]

    def head(index):
        offset = pl.multiple_of(lax.rem(index, piece_heads) * HEAD_DIM, HEAD_DIM)
        return packed_ref[index // piece_heads, :, pl.ds(offset, HEAD_DIM)]

    for u in range(2 * ratio):
        turned = spun(head(group * 2 * ratio + u).astype(jnp.float32), cosine, sine)
        spun_ref[:, u * HEAD_DIM : (u + 1) * HEAD_DIM] = turned.astype(jnp.bfloat16).astype(jnp.float32)
    scale = 1.0 / math.sqrt(HEAD_DIM)
    pairs = rows // 2
    group_rows = 2 * STEPS * ratio
    count = pairs * group_rows
    place = lax.broadcasted_iota(jnp.int32, (count, 1), 0)
    token_of = (place // group_rows) * (2 * STEPS) + place % (2 * STEPS)
    row_of = token_of // STEPS
    live = jnp.zeros((count, 1), jnp.int32)
    for row in range(rows):
        live = jnp.where(row_of == row, length_ref[block * rows + row], live)
    old_start = (row_of % 2) * cached
    old_column = lax.broadcasted_iota(jnp.int32, (count, 2 * cached), 1) - old_start
    old_kept = (old_column >= 0) & (old_column < live)
    new_column = lax.broadcasted_iota(jnp.int32, (count, tokens), 1)
    new_kept = (new_column >= row_of * STEPS) & (new_column <= token_of)
    contract_last = (((1,), (1,)), ((), ()))

    def columns(half, u):
        return slice((half * ratio + u) * HEAD_DIM, (half * ratio + u + 1) * HEAD_DIM)

    for half in range(2):
        lanes = slice(half * HEAD_DIM, (half + 1) * HEAD_DIM)
        new_keys = spun(head(HEADS + group * 2 + half).astype(jnp.float32), cosine, sine).astype(jnp.bfloat16)
        new_values = head(HEADS + KV_HEADS + group * 2 + half)
        queries = [
            jnp.concatenate(
                [spun_ref[2 * STEPS * pair : 2 * STEPS * (pair + 1), columns(half, u)] for u in range(ratio)],
                axis=0,
            )
            for pair in range(pairs)
        ]
        old_scores = jnp.concatenate(
            [
                lax.dot_general(
                    queries[pair].astype(jnp.bfloat16),
                    keys_ref[2 * pair : 2 * pair + 2, :, lanes].reshape(2 * cached, HEAD_DIM),
                    contract_last,
                    preferred_element_type=jnp.float32,
                )
                for pair in range(pairs)
            ],
            axis=0,
        )
        new_scores = lax.dot_general(
            jnp.concatenate(queries, axis=0).astype(jnp.bfloat16),
            new_keys,
            contract_last,
            preferred_element_type=jnp.float32,
        )
        old_scores = jnp.where(old_kept, old_scores * scale, -1e30)
        new_scores = jnp.where(new_kept, new_scores * scale, -1e30)
        peak = jnp.maximum(
            jnp.max(old_scores, axis=1, keepdims=True), jnp.max(new_scores, axis=1, keepdims=True)
        )
        old_exp = jnp.exp(old_scores - peak)
        new_exp = jnp.exp(new_scores - peak)
        share = 1.0 / (jnp.sum(old_exp, axis=1, keepdims=True) + jnp.sum(new_exp, axis=1, keepdims=True))
        old_weights = old_exp * share
        fresh = jnp.dot(
            (new_exp * share).astype(jnp.bfloat16), new_values, preferred_element_type=jnp.float32
        )
        for pair in range(pairs):
            part = slice(pair * group_rows, (pair + 1) * group_rows)
            total = fresh[part] + jnp.dot(
                old_weights[part].astype(jnp.bfloat16),
                values_ref[2 * pair : 2 * pair + 2, :, lanes].reshape(2 * cached, HEAD_DIM),
                preferred_element_type=jnp.float32,
            )
            for u in range(ratio):
                sum_ref[2 * STEPS * pair : 2 * STEPS * (pair + 1), columns(half, u)] = total[
                    2 * STEPS * u : 2 * STEPS * (u + 1)
                ]
    out_ref[...] = sum_ref[...].astype(jnp.bfloat16)


def attend_slots(pieces, keys, values, lengths, rep_index):
    rows, cached = keys.shape[0], keys.shape[1]
    block_rows = 8
    tokens = block_rows * STEPS
    positions = (lengths[:, None] + jnp.arange(STEPS, dtype=jnp.int32)[None, :]).reshape(-1)
    frequency = jnp.power(
        jnp.float32(ROPE_BASE), -jnp.arange(0, HEAD_DIM, 2, dtype=jnp.float32) / HEAD_DIM
    )
    angles = positions.astype(jnp.float32)[:, None] * frequency[None, :]
    cosine, sine = jnp.cos(angles), jnp.sin(angles)
    cosine = jnp.concatenate([cosine, cosine], axis=1)
    sine = jnp.concatenate([-sine, sine], axis=1)
    width = QDIM // 4
    pair_width = KVD // 4
    return pl.pallas_call(
        attention_kernel,
        out_shape=jax.ShapeDtypeStruct((rows * STEPS, QDIM), jnp.bfloat16),
        grid_spec=pltpu.PrefetchScalarGridSpec(
            num_scalar_prefetch=2,
            grid=(rows // block_rows, 4),
            in_specs=[
                pl.BlockSpec((pieces.shape[0], tokens, pieces.shape[2]), lambda i, j, p, n: (0, i, 0)),
                pl.BlockSpec((tokens, HEAD_DIM), lambda i, j, p, n: (i, 0)),
                pl.BlockSpec((tokens, HEAD_DIM), lambda i, j, p, n: (i, 0)),
                pl.BlockSpec((block_rows, cached, pair_width), lambda i, j, p, n: (i, 0, p[0] ^ j)),
                pl.BlockSpec((block_rows, cached, pair_width), lambda i, j, p, n: (i, 0, p[0] ^ j)),
            ],
            out_specs=pl.BlockSpec((tokens, width), lambda i, j, p, n: (i, j)),
            scratch_shapes=[
                pltpu.VMEM((tokens, width), jnp.float32),
                pltpu.VMEM((tokens, width), jnp.float32),
            ],
        ),
        cost_estimate=pl.CostEstimate(flops=2_000_000_000, bytes_accessed=10_000_000, transcendentals=2_000_000),
        name="attend_slots",
    )(rep_index.astype(jnp.int32).reshape(1), lengths, pieces, cosine, sine, keys, values)


def product_kernel(blocks, groups, has_buffer, order_ref, *refs):
    refs = list(refs)
    row_refs = [refs.pop(0) for _ in range(blocks)]
    weight_refs = [refs.pop(0) for _ in range(4 * groups)]
    bias_ref = refs.pop(0)
    if has_buffer:
        refs.pop(0)
    out_ref, rows_vmem, weights_vmem, total, out_vmem, row_sem, weight_sem, out_sem = refs
    height = row_refs[0].shape[0]
    _, depth = weight_refs[0].shape

    def row_copy(m, j):
        columns = pl.ds(j * depth, depth) if isinstance(j, int) else pl.ds(pl.multiple_of(j * depth, depth), depth)
        return pltpu.make_async_copy(
            row_refs[m].at[:, columns],
            rows_vmem.at[pl.ds(m * height, height), columns],
            row_sem.at[m, j],
        )

    def weight_copy(i):
        return pltpu.make_async_copy(weight_refs[i], weights_vmem.at[i], weight_sem.at[i])

    for j in range(4):
        weight_copy(j).start()
        for m in range(blocks):
            row_copy(m, j).start()
    for i in range(4, 4 * groups):
        weight_copy(i).start()
    total[...] = jnp.zeros_like(total)

    @pl.loop(0, 4 * groups)
    def _(i):
        pltpu.make_async_copy(weight_refs[0], weights_vmem.at[i], weight_sem.at[i]).wait()

        @pl.when(i < 4)
        def _():
            for m in range(blocks):
                row_copy(m, i).wait()

        columns = pl.ds(pl.multiple_of(lax.rem(i, 4) * depth, depth), depth)
        total[i // 4] += lax.dot_general(
            rows_vmem[:, columns],
            weights_vmem[i],
            (((1,), (1,)), ((), ())),
            preferred_element_type=jnp.float32,
        )

    low_first = order_ref[blocks] == 1
    mine = total[0] + bias_ref[0:1]
    others = total[1] + bias_ref[1:2]

    @pl.when(low_first)
    def _():
        out_vmem[...] = jnp.concatenate([mine, others], axis=1).astype(jnp.bfloat16)

    @pl.when(jnp.logical_not(low_first))
    def _():
        out_vmem[...] = jnp.concatenate([others, mine], axis=1).astype(jnp.bfloat16)

    out_copies = [
        pltpu.make_async_copy(out_vmem.at[pl.ds(m * height, height)], out_ref.at[order_ref[m]], out_sem.at[m])
        for m in range(blocks)
    ]
    for copy in out_copies:
        copy.start()
    for copy in out_copies:
        copy.wait()


def product(row_blocks, weights, bias, order, buffer=None):
    blocks = len(row_blocks)
    groups = len(weights) // 4
    height, full = row_blocks[0].shape
    width, depth = weights[0].shape
    anywhere = pl.BlockSpec(memory_space=pl.ANY)
    inside = pl.BlockSpec(memory_space=pltpu.VMEM)
    operands = list(row_blocks) + list(weights) + [bias]
    specs = [anywhere] * (len(operands) - 1) + [inside]
    aliases = {}
    if buffer is not None:
        operands.append(buffer)
        specs.append(anywhere)
        aliases = {len(operands): 0}
    out_shape = jax.ShapeDtypeStruct((8, height, 2 * width), jnp.bfloat16)
    return pl.pallas_call(
        functools.partial(product_kernel, blocks, groups, buffer is not None),
        out_shape=out_shape,
        grid_spec=pltpu.PrefetchScalarGridSpec(
            num_scalar_prefetch=1,
            grid=(),
            in_specs=specs,
            out_specs=anywhere,
            scratch_shapes=[
                pltpu.VMEM((blocks * height, full), jnp.bfloat16),
                pltpu.VMEM((4 * groups, width, depth), jnp.bfloat16),
                pltpu.VMEM((groups, blocks * height, width), jnp.float32),
                pltpu.VMEM((blocks * height, 2 * width), jnp.bfloat16),
                pltpu.SemaphoreType.DMA((blocks, 4)),
                pltpu.SemaphoreType.DMA((4 * groups,)),
                pltpu.SemaphoreType.DMA((blocks,)),
            ],
        ),
        input_output_aliases=aliases,
        cost_estimate=pl.CostEstimate(
            flops=2 * blocks * height * full * width * groups,
            bytes_accessed=2 * full * width * groups + 2 * blocks * height * full,
            transcendentals=0,
        ),
        name="product",
    )(order, *operands)


def body(qkv_versions, qkv_bias, o_versions, norm_gain, hidden, cache_keys, cache_values, lengths):
    trainer_side = lax.axis_index("role") == 0
    shard_index = lax.axis_index("shard")
    rep_index = lax.axis_index("rep")
    rep_total = lax.axis_size("rep")
    own_qkv = qkv_versions[0].T
    own_out = o_versions[0]
    states = hidden[0].astype(jnp.float32)
    rows = states.shape[0]
    tokens = rows * STEPS
    near, far, low_first = owner_order(shard_index)
    normed = normalize(states, norm_gain[0]).reshape(tokens, D)
    qkv_slots = gather_weights(own_qkv)
    width = own_qkv.shape[0]
    bias = qkv_bias[0].astype(jnp.float32).reshape(1, -1)
    own_bias = lax.dynamic_slice_in_dim(bias, shard_index * width, width, 1)
    pair_bias = lax.dynamic_slice_in_dim(bias, (shard_index ^ 1) * width, width, 1)
    same, mirror = gather_rows(slot_columns(normed, rep_index))
    order = jnp.concatenate([near, far, low_first])
    spread = lax.all_to_all(own_out, "shard", split_axis=0, concat_axis=1, tiled=True)
    turned = rotate_columns(after(spread, same[3]))
    folded_out = lax.all_to_all(
        turned, "shard", split_axis=1, concat_axis=0, tiled=True
    )
    both_bias = jnp.concatenate([own_bias, pair_bias], axis=0)
    part = product(
        same + mirror, qkv_slots[0] + qkv_slots[1], both_bias, after(order, turned)
    )
    packed = to_owners(after(part, folded_out))
    out_slots = gather_weights(after(own_out.T, turned), part, packed)
    weights = out_slots[0] + out_slots[1]
    sent_out = shifted(after(folded_out, part), "role", 1)
    packed = after(packed, out_slots[2], *weights[:6])
    attended = attend_slots(packed, cache_keys[0], cache_values[0], lengths[0], rep_index)
    folded_qkv = rotate_column_part(
        (after(qkv_slots[0][0], attended),) + qkv_slots[0][1:], rep_index, rep_total
    )
    sent_qkv = shifted(folded_qkv, "role", 1)
    same, mirror = gather_rows(attended)
    no_bias = jnp.zeros((2, own_out.shape[1]), jnp.float32)
    part = product(same, weights, no_bias, jnp.concatenate([near, low_first]))
    part = product(mirror, weights, no_bias, jnp.concatenate([far, low_first]), buffer=part)
    sent_qkv, sent_out = after(sent_qkv, part), after(sent_out, part)
    projected = to_owners(part)
    projected = projected.transpose(1, 0, 2).reshape(rows, STEPS, D).astype(jnp.float32)
    layer_out = (states + projected).astype(jnp.bfloat16)[None]
    new_qkv = jnp.where(trainer_side, folded_qkv, sent_qkv)
    new_o = jnp.where(trainer_side, folded_out, sent_out)
    return (layer_out, new_qkv.T[None], new_o[None])


def solution(mesh):
    in_specs = (
        P("role", "rep", "shard"),
        P("role", None),
        P("role", "rep", "shard"),
        P("role", None),
        P("role", ("shard", "rep"), None, None),
        P("role", ("shard", "rep"), None, None),
        P("role", ("shard", "rep"), None, None),
        P("role", ("shard", "rep")),
    )
    out_specs = (
        P("role", ("shard", "rep"), None, None),
        P("role", "rep", "shard"),
        P("role", "rep", "shard"),
    )
    return jax.shard_map(body, mesh=mesh, in_specs=in_specs, out_specs=out_specs, check_vma=False)
```

profile of v0, /device:TPU:0, one launch (start us, length us, event | category | flops | bytes accessed | tf_op | source)
XLA Modules:
  0.0 235.7 jit_solution(9622897801914841064)
XLA Ops:
  0.7 1.5 reshape.168
  3.0 0.9 pad_maximum_fusion.refs_0_
  3.9 2.0 collective-permute-start
  5.9 2.1 collective-permute-start.1
  8.1 3.0 %collective-permute-start.3 = (bf16[64,5120]{1,0:T(8,128)(2,1)}, bf16[64,5120]{1,0:T(8,128)(2,1)}, u32[]{:S(2)}, u32[]{:S(2)}) collective-permute-start(bf16[64,5120]{1,0:T(8,128)(2,1)} %pad_maximum_fusion.refs_0_), channel_id=1, source_target_pairs={{0,12},{4,8},{8,4},{12,0},{16,28},{20,24},{24,20},{28,16},{32,44},... | collective-permute-start | bytes 1966088 | tf_op jit(solution)/shard_map/ppermute | solution.py:44
  11.1 1.5 collective-permute-start.8
  12.7 10.3 %collective-permute-done.refs_1_ = bf16[64,5120]{1,0:T(8,128)(2,1)S(1)} collective-permute-done((bf16[64,5120]{1,0:T(8,128)(2,1)}, bf16[64,5120]{1,0:T(8,128)(2,1)S(1)}, u32[]{:S(2)}, u32[]{:S(2)}) %collective-permute-start) | collective-permute-done | bytes 655392 | tf_op jit(solution)/shard_map/ppermute | solution.py:39
  23.0 0.8 copy-done.11
  23.8 0.9 copy-done.12
  24.7 0.9 broadcast_select_fusion.3
  26.0 11.8 %collective-permute-done.8.refs_10_.refs_2_ = bf16[448,1280]{1,0:T(8,128)(2,1)} collective-permute-done((bf16[448,1280]{1,0:T(8,128)(2,1)}, bf16[448,1280]{1,0:T(8,128)(2,1)}, u32[]{:S(2)}, u32[]{:S(2)}) %collective-permute-start.8) | collective-permute-done | bytes 1146912 | tf_op jit(solution)/shard_map/ppermute | solution.py:53
  37.8 1.2 collective-permute-done.10.refs_12_
  39.1 1.4 broadcast_select_fusion
  40.4 0.6 collective-permute-start.12
  41.1 1.3 copy.33
  42.4 3.8 %all-to-all-start = ((bf16[16,80,320]{2,1,0:T(8,128)(2,1)}), bf16[16,80,320]{2,1,0:T(8,128)(2,1)S(1)}, u32[]{:S(2)}, u32[]{:S(2)}) async-start(bf16[16,80,320]{2,1,0:T(8,128)(2,1)} %bitcast.3), calls=%async_computation | async-start | bytes 1966080 | tf_op jit(solution)/shard_map/all_to_all | solution.py:509
  46.2 1.9 collective-permute-start.4
  49.1 1.4 collective-permute-start.5
  50.5 22.0 %collective-permute-done.4.refs_5_ = bf16[64,5120]{1,0:T(8,128)(2,1)} collective-permute-done((bf16[64,5120]{1,0:T(8,128)(2,1)}, bf16[64,5120]{1,0:T(8,128)(2,1)}, u32[]{:S(2)}, u32[]{:S(2)}) %collective-permute-start.4) | collective-permute-done | bytes 655392 | tf_op jit(solution)/shard_map/ppermute | solution.py:39
  72.5 2.7 %collective-permute-start.6 = (bf16[64,5120]{1,0:T(8,128)(2,1)}, bf16[64,5120]{1,0:T(8,128)(2,1)}, u32[]{:S(2)}, u32[]{:S(2)}) collective-permute-start(bf16[64,5120]{1,0:T(8,128)(2,1)} %collective-permute-done.2.refs_3_), channel_id=1, source_target_pairs={{0,12},{4,8},{8,4},{12,0},{16,28},{20,24},{24,20},{28,16},{32,44},... | collective-permute-start | bytes 1966088 | tf_op jit(solution)/shard_map/ppermute | solution.py:44
  75.5 0.8 all_to_all.35
  76.5 0.6 fusion.5
  77.1 2.4 %multiply_convert_fusion = bf16[40,80,128]{2,0,1:T(8,128)(2,1)} fusion(f32[40,40,1]{0,1,2:T(8,128)S(1)} %reshape.172, f32[80,40,128]{2,1,0:T(8,128)S(1)} %fusion.5), kind=kOutput, calls=%fused_computation | convolution fusion | flops 197427200 | bytes 2464000 | tf_op jit(solution)/shard_map/may,ax->mxy/dot_general | solution.py:230
  80.1 9.3 %collective-permute-done.6.refs_7_ = bf16[64,5120]{1,0:T(8,128)(2,1)} collective-permute-done((bf16[64,5120]{1,0:T(8,128)(2,1)}, bf16[64,5120]{1,0:T(8,128)(2,1)}, u32[]{:S(2)}, u32[]{:S(2)}) %collective-permute-start.6) | collective-permute-done | bytes 655392 | tf_op jit(solution)/shard_map/ppermute | solution.py:44
  89.9 0.6 pad_add_fusion.1.order_ref
  90.6 0.6 pad_maximum_fusion.4.refs_16_
  91.2 2.0 convert_element_type.106
  93.2 1.1 copy.35
  94.3 5.5 %all-to-all-start.1 = ((bf16[80,16,320]{2,0,1:T(8,128)(2,1)}), bf16[80,16,320]{2,0,1:T(8,128)(2,1)S(1)}, u32[]{:S(2)}, u32[]{:S(2)}) async-start(bf16[80,16,320]{2,0,1:T(8,128)(2,1)} %copy.35), calls=%async_computation.1 | async-start | bytes 1966080 | tf_op jit(solution)/shard_map/all_to_all | solution.py:511
  100.2 12.7 %product.3 = bf16[8,64,896]{2,1,0:T(8,128)(2,1)} custom-call(s32[9]{0:T(128)} %pad_add_fusion.1.order_ref, bf16[64,5120]{1,0:T(8,128)(2,1)} %pad_maximum_fusion.refs_0_, bf16[64,5120]{1,0:T(8,128)(2,1)} %copy-done.11, bf16[64,5120]{1,0:T(8,128)(2,1)} %copy-done.12, bf16[64,5120]{1,0:T(8,128)(2,1)} %collective-permute-done.2.refs_3_, ...), custom_call_target="tpu_custom_call" | custom-call | flops 4697620480 | bytes 14417920 | tf_op jit(solution)/shard_map/product/pallas_call | solution.py:462
  112.9 1.1 broadcast_select_fusion.1
  114.1 2.1 collective-permute-start.18
  116.2 3.3 %all-to-all-done.1 = bf16[80,16,320]{2,0,1:T(8,128)(2,1)S(1)} async-done(((bf16[80,16,320]{2,0,1:T(8,128)(2,1)}), bf16[80,16,320]{2,0,1:T(8,128)(2,1)S(1)}, u32[]{:S(2)}, u32[]{:S(2)}) %all-to-all-start.1) | async-done | bytes 819232 | tf_op jit(solution)/shard_map/all_to_all | solution.py:511
  119.4 4.4 %all-to-all-start.2 = ((bf16[8,64,896]{2,1,0:T(8,128)(2,1)}), bf16[8,64,896]{2,1,0:T(8,128)(2,1)}, u32[]{:S(2)}, u32[]{:S(2)}) async-start(bf16[8,64,896]{2,1,0:T(8,128)(2,1)} %product.3), calls=%async_computation.2 | async-start | bytes 1835008 | tf_op jit(solution)/shard_map/all_to_all | solution.py:137
  124.2 0.7 pad_maximum_fusion.1
  124.9 13.3 %all-to-all-done.2.packed_ref = bf16[8,64,896]{2,1,0:T(8,128)(2,1)} async-done(((bf16[8,64,896]{2,1,0:T(8,128)(2,1)}), bf16[8,64,896]{2,1,0:T(8,128)(2,1)}, u32[]{:S(2)}, u32[]{:S(2)}) %all-to-all-start.2) | async-done | bytes 917536 | tf_op jit(solution)/shard_map/all_to_all | solution.py:137
  138.2 12.3 %attend_slots.1.refs_0_ = bf16[64,5120]{1,0:T(8,128)(2,1)} custom-call(s32[1]{0:T(128)} %bitcast.1.part_ref, s32[16]{0:T(128)} %bitcast.56, bf16[8,64,896]{2,1,0:T(8,128)(2,1)} %all-to-all-done.2.packed_ref, f32[64,128]{1,0:T(8,128)} %get-tuple-element.55.cosine_ref, f32[64,128]{1,0:T(8,128)} %get-tuple-element.56.sine_ref, bf16[16,128,1024]{2,1,0:T(8,128)(2,1)} %bitcast.49, ...), custom_call_target="tpu_custom_call" | custom-call | flops 2000000000 | bytes 10000000 | tf_op jit(solution)/shard_map/attend_slots/pallas_call | solution.py:354
  150.6 3.2 %collective-permute-start.22 = (bf16[64,5120]{1,0:T(8,128)(2,1)}, bf16[64,5120]{1,0:T(8,128)(2,1)S(1)}, u32[]{:S(2)}, u32[]{:S(2)}) collective-permute-start(bf16[64,5120]{1,0:T(8,128)(2,1)} %attend_slots.1.refs_0_), channel_id=1, source_target_pairs={{0,48},{4,52},{8,56},{12,60},{16,0},{20,4},{24,8},{28,12},{32,16},... | collective-permute-start | bytes 1966088 | tf_op jit(solution)/shard_map/ppermute | solution.py:39
  153.8 0.9 collective-permute-start.20
  154.7 11.5 %collective-permute-done.21.refs_1_ = bf16[64,5120]{1,0:T(8,128)(2,1)S(1)} collective-permute-done((bf16[64,5120]{1,0:T(8,128)(2,1)}, bf16[64,5120]{1,0:T(8,128)(2,1)S(1)}, u32[]{:S(2)}, u32[]{:S(2)}) %collective-permute-start.21) | collective-permute-done | bytes 655392 | tf_op jit(solution)/shard_map/ppermute | solution.py:39
  166.1 1.0 broadcast_select_fusion.2
  167.4 0.7 copy.37.outer_ref
  168.1 0.7 fusion.4.inner_ref
  168.8 1.3 copy.38
  170.1 5.6 %collective-permute-start.29 = (bf16[1280,320]{0,1:T(8,128)(2,1)}, bf16[1280,320]{0,1:T(8,128)(2,1)}, u32[]{:S(2)}, u32[]{:S(2)}) collective-permute-start(bf16[1280,320]{0,1:T(8,128)(2,1)} %copy.38), channel_id=1, source_target_pairs={{0,64},{1,65},{2,66},{3,67},{4,68},{5,69},{6,70},{7,71},{8,72},{9,... | collective-permute-start | bytes 2457608 | tf_op jit(solution)/shard_map/ppermute | solution.py:33
  175.7 3.6 %collective-permute-done.23.refs_3_ = bf16[64,5120]{1,0:T(8,128)(2,1)} collective-permute-done((bf16[64,5120]{1,0:T(8,128)(2,1)}, bf16[64,5120]{1,0:T(8,128)(2,1)}, u32[]{:S(2)}, u32[]{:S(2)}) %collective-permute-start.23) | collective-permute-done | bytes 655392 | tf_op jit(solution)/shard_map/ppermute | solution.py:68
  179.3 3.2 %collective-permute-start.25 = (bf16[64,5120]{1,0:T(8,128)(2,1)}, bf16[64,5120]{1,0:T(8,128)(2,1)S(1)}, u32[]{:S(2)}, u32[]{:S(2)}) collective-permute-start(bf16[64,5120]{1,0:T(8,128)(2,1)} %collective-permute-done.20.refs_0_), channel_id=1, source_target_pairs={{0,48},{4,52},{8,56},{12,60},{16,0},{20,4},{24,8},{28,12},{32,16},... | collective-permute-start | bytes 1966088 | tf_op jit(solution)/shard_map/ppermute | solution.py:39
  182.5 0.7 collective-permute-start.26
  183.2 8.9 %fold_part.1 = bf16[448,1280]{1,0:T(8,128)(2,1)} custom-call(f32[40,10]{1,0:T(8,128)} %copy.37.outer_ref, bf16[128,128]{1,0:T(8,128)(2,1)} %fusion.4.inner_ref, bf16[448,1280]{1,0:T(8,128)(2,1)} %bitcast.9.refs_8_.refs_0_, bf16[448,1280]{1,0:T(8,128)(2,1)} %collective-permute-done.7.refs_9_.refs_1_, ...), custom_call_target="tpu_custom_call" | custom-call | flops 4000000000 | bytes 6000000 | tf_op jit(solution)/shard_map/fold_part/pallas_call | solution.py:208
  192.0 6.3 %collective-permute-start.28 = (bf16[448,1280]{1,0:T(8,128)(2,1)}, bf16[448,1280]{1,0:T(8,128)(2,1)}, u32[]{:S(2)}, u32[]{:S(2)}) collective-permute-start(bf16[448,1280]{1,0:T(8,128)(2,1)} %fold_part.1), channel_id=1, source_target_pairs={{0,64},{1,65},{2,66},{3,67},{4,68},{5,69},{6,70},{7,71},{8,72},{9,... | collective-permute-start | bytes 3440648 | tf_op jit(solution)/shard_map/ppermute | solution.py:33
  198.3 0.6 pad_add_fusion.2.order_ref
  198.9 0.6 pad_add_fusion.order_ref
  200.1 8.6 %product.4.refs_13_ = bf16[8,64,640]{2,1,0:T(8,128)(2,1)} custom-call(s32[5]{0:T(128)} %pad_add_fusion.2.order_ref, bf16[64,5120]{1,0:T(8,128)(2,1)} %attend_slots.1.refs_0_, bf16[64,5120]{1,0:T(8,128)(2,1)} %copy-done.6, bf16[64,5120]{1,0:T(8,128)(2,1)} %copy-done.7, bf16[64,5120]{1,0:T(8,128)(2,1)} %collective-permute-done.23.refs_3_, ...), custom_call_target="tpu_custom_call" | custom-call | flops 1677721600 | bytes 9175040 | tf_op jit(solution)/shard_map/product/pallas_call | solution.py:462
  208.7 0.8 copy-done.9
  209.8 8.6 %product.5 = bf16[8,64,640]{2,1,0:T(8,128)(2,1)} custom-call(s32[5]{0:T(128)} %pad_add_fusion.order_ref, bf16[64,5120]{1,0:T(8,128)(2,1)} %collective-permute-done.20.refs_0_, bf16[64,5120]{1,0:T(8,128)(2,1)} %copy-done.9, bf16[64,5120]{1,0:T(8,128)(2,1)} %copy-done.10, ...), custom_call_target="tpu_custom_call", output_to_operand_aliasing={{}: (14, {})} | custom-call | flops 1677721600 | bytes 9175040 | tf_op jit(solution)/shard_map/product/pallas_call | solution.py:462
  218.4 3.8 %all-to-all-start.3 = ((bf16[8,64,640]{2,1,0:T(8,128)(2,1)}), bf16[8,64,640]{2,1,0:T(8,128)(2,1)S(1)}, u32[]{:S(2)}, u32[]{:S(2)}) async-start(bf16[8,64,640]{2,1,0:T(8,128)(2,1)} %product.5), calls=%async_computation.3 | async-start | bytes 1310720 | tf_op jit(solution)/shard_map/all_to_all | solution.py:137
  222.2 1.6 copy.39
  223.7 1.2 select_bitcast_fusion.1
  224.9 2.3 copy.40
  227.2 1.1 select_bitcast_fusion
  228.3 4.2 %all-to-all-done.3 = bf16[8,64,640]{2,1,0:T(8,128)(2,1)S(1)} async-done(((bf16[8,64,640]{2,1,0:T(8,128)(2,1)}), bf16[8,64,640]{2,1,0:T(8,128)(2,1)S(1)}, u32[]{:S(2)}, u32[]{:S(2)}) %all-to-all-start.3) | async-done | bytes 655392 | tf_op jit(solution)/shard_map/all_to_all | solution.py:137
  232.6 0.8 copy.36
  233.9 0.6 copy-done.4
  234.5 1.2 add_convert_fusion
  (103 shorter events, 6.4 us)
Async XLA Ops:
  0.6 1.5 copy-start.3
  0.7 2.0 copy-start.14
  3.9 19.1 %collective-permute-start = (bf16[64,5120]{1,0:T(8,128)(2,1)}, bf16[64,5120]{1,0:T(8,128)(2,1)S(1)}, u32[]{:S(2)}, u32[]{:S(2)}) collective-permute-start(bf16[64,5120]{1,0:T(8,128)(2,1)} %pad_maximum_fusion.refs_0_), channel_id=1, source_target_pairs={{0,16},{4,20},{8,24},{12,28},{16,32},{20,36},{24,40},{28,44},{32,4... | collective-permute-start | bytes 1966088 | tf_op jit(solution)/shard_map/ppermute | solution.py:39
  5.9 17.1 %collective-permute-start.1 = (bf16[64,5120]{1,0:T(8,128)(2,1)}, bf16[64,5120]{1,0:T(8,128)(2,1)S(1)}, u32[]{:S(2)}, u32[]{:S(2)}) collective-permute-start(bf16[64,5120]{1,0:T(8,128)(2,1)} %pad_maximum_fusion.refs_0_), channel_id=1, source_target_pairs={{0,48},{4,52},{8,56},{12,60},{16,0},{20,4},{24,8},{28,12},{32,16},... | collective-permute-start | bytes 1966088 | tf_op jit(solution)/shard_map/ppermute | solution.py:39
  8.1 38.1 %collective-permute-start.3 = (bf16[64,5120]{1,0:T(8,128)(2,1)}, bf16[64,5120]{1,0:T(8,128)(2,1)}, u32[]{:S(2)}, u32[]{:S(2)}) collective-permute-start(bf16[64,5120]{1,0:T(8,128)(2,1)} %pad_maximum_fusion.refs_0_), channel_id=1, source_target_pairs={{0,12},{4,8},{8,4},{12,0},{16,28},{20,24},{24,20},{28,16},{32,44},... | collective-permute-start | bytes 1966088 | tf_op jit(solution)/shard_map/ppermute | solution.py:44
  11.1 26.8 %collective-permute-start.8 = (bf16[448,1280]{1,0:T(8,128)(2,1)}, bf16[448,1280]{1,0:T(8,128)(2,1)}, u32[]{:S(2)}, u32[]{:S(2)}) collective-permute-start(bf16[448,1280]{1,0:T(8,128)(2,1)} %bitcast.9.refs_8_.refs_0_), channel_id=1, source_target_pairs={{0,2},{1,3},{2,0},{3,1},{4,6},{5,7},{6,4},{7,5},{8,10},{9,11},{10,... | collective-permute-start | bytes 3440648 | tf_op jit(solution)/shard_map/ppermute | solution.py:53
  12.6 26.5 %collective-permute-start.10 = (bf16[448,1280]{1,0:T(8,128)(2,1)}, bf16[448,1280]{1,0:T(8,128)(2,1)}, u32[]{:S(2)}, u32[]{:S(2)}) collective-permute-start(bf16[448,1280]{1,0:T(8,128)(2,1)} %bitcast.9.refs_8_.refs_0_), channel_id=1, source_target_pairs={{0,4},{4,0},{8,12},{12,8},{16,20},{20,16},{24,28},{28,24},{32,36},... | collective-permute-start | bytes 3440648 | tf_op jit(solution)/shard_map/ppermute | solution.py:49
  23.0 0.8 copy-start.11
  23.0 26.1 %collective-permute-start.7 = (bf16[448,1280]{1,0:T(8,128)(2,1)}, bf16[448,1280]{1,0:T(8,128)(2,1)}, u32[]{:S(2)}, u32[]{:S(2)}) collective-permute-start(bf16[448,1280]{1,0:T(8,128)(2,1)} %bitcast.9.refs_8_.refs_0_), channel_id=1, source_target_pairs={{0,1},{1,0},{2,3},{3,2},{4,5},{5,4},{6,7},{7,6},{8,9},{9,8},{10,11... | collective-permute-start | bytes 3440648 | tf_op jit(solution)/shard_map/ppermute | solution.py:57
  23.8 0.9 copy-start.12
  25.6 15.5 %copy-start = (bf16[1,1280,320]{1,2,0:T(8,128)(2,1)S(1)}, bf16[1,1280,320]{1,2,0:T(8,128)(2,1)}, u32[]{:S(2)}) copy-start(bf16[1,1280,320]{1,2,0:T(8,128)(2,1)} %param.13) | copy-start | bytes 2457604
  25.6 20.6 %collective-permute-start.2 = (bf16[64,5120]{1,0:T(8,128)(2,1)}, bf16[64,5120]{1,0:T(8,128)(2,1)}, u32[]{:S(2)}, u32[]{:S(2)}) collective-permute-start(bf16[64,5120]{1,0:T(8,128)(2,1)} %broadcast_select_fusion.3), channel_id=1, source_target_pairs={{0,16},{1,49},{2,18},{3,51},{4,20},{5,53},{6,22},{7,55},{8,24},{9,... | collective-permute-start | bytes 1966088 | tf_op jit(solution)/shard_map/ppermute | solution.py:68
  40.4 34.8 %collective-permute-start.12 = (bf16[448,1280]{1,0:T(8,128)(2,1)S(1)}, bf16[448,1280]{1,0:T(8,128)(2,1)}, u32[]{:S(2)}, u32[]{:S(2)}) collective-permute-start(bf16[448,1280]{1,0:T(8,128)(2,1)S(1)} %broadcast_select_fusion), channel_id=1, source_target_pairs={{0,2},{1,5},{2,0},{3,7},{4,6},{5,1},{6,4},{7,3},{8,10},{9,13},{10,... | collective-permute-start | bytes 3440648 | tf_op jit(solution)/shard_map/ppermute | solution.py:68
  42.3 5.9 %copy-start.18 = (f32[1,20]{1,0:T(1,128)S(1)}, f32[1,20]{1,0:T(1,128)}, u32[]{:S(2)}) copy-start(f32[1,20]{1,0:T(1,128)} %constant.189.clone.1) | copy-start | bytes 244
  42.3 6.1 %copy-start.16 = (f32[2,2]{0,1:T(2,128)S(1)}, f32[2,2]{0,1:T(2,128)}, u32[]{:S(2)}) copy-start(f32[2,2]{0,1:T(2,128)} %constant.213.clone) | copy-start | bytes 52
  42.3 32.9 %copy-start.17 = (s32[4]{0:T(128)S(1)}, s32[4]{0:T(128)}, u32[]{:S(2)}) copy-start(s32[4]{0:T(128)} %constant.212.clone) | copy-start | bytes 52
  42.4 33.0 %all-to-all-start = ((bf16[16,80,320]{2,1,0:T(8,128)(2,1)}), bf16[16,80,320]{2,1,0:T(8,128)(2,1)S(1)}, u32[]{:S(2)}, u32[]{:S(2)}) async-start(bf16[16,80,320]{2,1,0:T(8,128)(2,1)} %bitcast.3), calls=%async_computation | async-start | bytes 1966080 | tf_op jit(solution)/shard_map/all_to_all | solution.py:509
  46.2 26.3 %collective-permute-start.4 = (bf16[64,5120]{1,0:T(8,128)(2,1)}, bf16[64,5120]{1,0:T(8,128)(2,1)}, u32[]{:S(2)}, u32[]{:S(2)}) collective-permute-start(bf16[64,5120]{1,0:T(8,128)(2,1)} %collective-permute-done.3.refs_4_), channel_id=1, source_target_pairs={{0,16},{4,20},{8,24},{12,28},{16,32},{20,36},{24,40},{28,44},{32,4... | collective-permute-start | bytes 1966088 | tf_op jit(solution)/shard_map/ppermute | solution.py:39
  48.5 51.4 %collective-permute-start.9 = (bf16[448,1280]{1,0:T(8,128)(2,1)}, bf16[448,1280]{1,0:T(8,128)(2,1)}, u32[]{:S(2)}, u32[]{:S(2)}) collective-permute-start(bf16[448,1280]{1,0:T(8,128)(2,1)} %collective-permute-done.8.refs_10_.refs_2_), channel_id=1, source_target_pairs={{0,1},{1,0},{2,3},{3,2},{4,5},{5,4},{6,7},{7,6},{8,9},{9,8},{10,11... | collective-permute-start | bytes 3440648 | tf_op jit(solution)/shard_map/ppermute | solution.py:57
  48.6 51.5 %collective-permute-start.11 = (bf16[448,1280]{1,0:T(8,128)(2,1)}, bf16[448,1280]{1,0:T(8,128)(2,1)}, u32[]{:S(2)}, u32[]{:S(2)}) collective-permute-start(bf16[448,1280]{1,0:T(8,128)(2,1)} %collective-permute-done.10.refs_12_), channel_id=1, source_target_pairs={{0,1},{1,0},{2,3},{3,2},{4,5},{5,4},{6,7},{7,6},{8,9},{9,8},{10,11... | collective-permute-start | bytes 3440648 | tf_op jit(solution)/shard_map/ppermute | solution.py:57
  49.1 30.4 %collective-permute-start.5 = (bf16[64,5120]{1,0:T(8,128)(2,1)}, bf16[64,5120]{1,0:T(8,128)(2,1)}, u32[]{:S(2)}, u32[]{:S(2)}) collective-permute-start(bf16[64,5120]{1,0:T(8,128)(2,1)} %collective-permute-done.3.refs_4_), channel_id=1, source_target_pairs={{0,48},{4,52},{8,56},{12,60},{16,0},{20,4},{24,8},{28,12},{32,16},... | collective-permute-start | bytes 1966088 | tf_op jit(solution)/shard_map/ppermute | solution.py:39
  72.5 16.8 %collective-permute-start.6 = (bf16[64,5120]{1,0:T(8,128)(2,1)}, bf16[64,5120]{1,0:T(8,128)(2,1)}, u32[]{:S(2)}, u32[]{:S(2)}) collective-permute-start(bf16[64,5120]{1,0:T(8,128)(2,1)} %collective-permute-done.2.refs_3_), channel_id=1, source_target_pairs={{0,12},{4,8},{8,4},{12,0},{16,28},{20,24},{24,20},{28,16},{32,44},... | collective-permute-start | bytes 1966088 | tf_op jit(solution)/shard_map/ppermute | solution.py:44
  75.2 25.0 %collective-permute-start.13 = (bf16[448,1280]{1,0:T(8,128)(2,1)}, bf16[448,1280]{1,0:T(8,128)(2,1)}, u32[]{:S(2)}, u32[]{:S(2)}) collective-permute-start(bf16[448,1280]{1,0:T(8,128)(2,1)} %collective-permute-done.12.refs_14_), channel_id=1, source_target_pairs={{0,1},{1,0},{2,3},{3,2},{4,5},{5,4},{6,7},{7,6},{8,9},{9,8},{10,11... | collective-permute-start | bytes 3440648 | tf_op jit(solution)/shard_map/ppermute | solution.py:57
  77.1 12.8 %copy-start.13 = (bf16[1,7168]{1,0:T(2,128)(2,1)S(1)}, bf16[1,7168]{1,0:T(2,128)(2,1)}, u32[]{:S(2)}) copy-start(bf16[1,7168]{1,0:T(2,128)(2,1)} %param.12) | copy-start | bytes 43012
  79.5 33.4 %collective-permute-start.14 = (bf16[320,1280]{1,0:T(8,128)(2,1)S(1)}, bf16[320,1280]{1,0:T(8,128)(2,1)S(1)}, u32[]{:S(2)}, u32[]{:S(2)}) collective-permute-start(bf16[320,1280]{1,0:T(8,128)(2,1)S(1)} %bitcast.46), channel_id=1, source_target_pairs={{0,2},{1,3},{2,0},{3,1},{4,6},{5,7},{6,4},{7,5},{8,10},{9,11},{10,... | collective-permute-start | bytes 2457608 | tf_op jit(solution)/shard_map/ppermute | solution.py:53
  89.3 23.6 %collective-permute-start.15 = (bf16[320,1280]{1,0:T(8,128)(2,1)S(1)}, bf16[320,1280]{1,0:T(8,128)(2,1)S(1)}, u32[]{:S(2)}, u32[]{:S(2)}) collective-permute-start(bf16[320,1280]{1,0:T(8,128)(2,1)S(1)} %bitcast.47), channel_id=1, source_target_pairs={{0,4},{4,0},{8,12},{12,8},{16,20},{20,16},{24,28},{28,24},{32,36},... | collective-permute-start | bytes 2457608 | tf_op jit(solution)/shard_map/ppermute | solution.py:49
  94.3 25.1 %all-to-all-start.1 = ((bf16[80,16,320]{2,0,1:T(8,128)(2,1)}), bf16[80,16,320]{2,0,1:T(8,128)(2,1)S(1)}, u32[]{:S(2)}, u32[]{:S(2)}) async-start(bf16[80,16,320]{2,0,1:T(8,128)(2,1)} %copy.35), calls=%async_computation.1 | async-start | bytes 1966080 | tf_op jit(solution)/shard_map/all_to_all | solution.py:511
  99.9 25.1 %collective-permute-start.17 = (bf16[320,1280]{1,0:T(8,128)(2,1)S(1)}, bf16[320,1280]{1,0:T(8,128)(2,1)}, u32[]{:S(2)}, u32[]{:S(2)}) collective-permute-start(bf16[320,1280]{1,0:T(8,128)(2,1)S(1)} %bitcast.48), channel_id=1, source_target_pairs={{0,1},{1,0},{2,3},{3,2},{4,5},{5,4},{6,7},{7,6},{8,9},{9,8},{10,11... | collective-permute-start | bytes 2457608 | tf_op jit(solution)/shard_map/ppermute | solution.py:57
  112.9 6.5 %copy-start.1 = (bf16[320,1280]{1,0:T(8,128)(2,1)}, bf16[320,1280]{1,0:T(8,128)(2,1)S(1)}, u32[]{:S(2)}) copy-start(bf16[320,1280]{1,0:T(8,128)(2,1)S(1)} %collective-permute-done.14.refs_6_) | copy-start | bytes 2457604
  112.9 6.5 %copy-start.2 = (bf16[320,1280]{1,0:T(8,128)(2,1)}, bf16[320,1280]{1,0:T(8,128)(2,1)S(1)}, u32[]{:S(2)}) copy-start(bf16[320,1280]{1,0:T(8,128)(2,1)S(1)} %collective-permute-done.15.refs_8_) | copy-start | bytes 2457604
  114.1 9.8 %copy-start.15 = (s32[1,16]{1,0:T(1,128)S(1)}, s32[1,16]{1,0:T(1,128)}, u32[]{:S(2)}) copy-start(s32[1,16]{1,0:T(1,128)} %param.18) | copy-start | bytes 196
  114.1 24.2 %collective-permute-start.16 = (bf16[320,1280]{1,0:T(8,128)(2,1)}, bf16[320,1280]{1,0:T(8,128)(2,1)}, u32[]{:S(2)}, u32[]{:S(2)}) collective-permute-start(bf16[320,1280]{1,0:T(8,128)(2,1)} %broadcast_select_fusion.1), channel_id=1, source_target_pairs={{0,2},{1,5},{2,0},{3,7},{4,6},{5,1},{6,4},{7,3},{8,10},{9,13},{10,... | collective-permute-start | bytes 2457608 | tf_op jit(solution)/shard_map/ppermute | solution.py:68
  114.1 24.2 %collective-permute-start.18 = (bf16[320,1280]{1,0:T(8,128)(2,1)S(1)}, bf16[320,1280]{1,0:T(8,128)(2,1)}, u32[]{:S(2)}, u32[]{:S(2)}) collective-permute-start(bf16[320,1280]{1,0:T(8,128)(2,1)S(1)} %collective-permute-done.14.refs_6_), channel_id=1, source_target_pairs={{0,1},{1,0},{2,3},{3,2},{4,5},{5,4},{6,7},{7,6},{8,9},{9,8},{10,11... | collective-permute-start | bytes 2457608 | tf_op jit(solution)/shard_map/ppermute | solution.py:57
  116.2 22.1 %collective-permute-start.19 = (bf16[320,1280]{1,0:T(8,128)(2,1)S(1)}, bf16[320,1280]{1,0:T(8,128)(2,1)}, u32[]{:S(2)}, u32[]{:S(2)}) collective-permute-start(bf16[320,1280]{1,0:T(8,128)(2,1)S(1)} %collective-permute-done.15.refs_8_), channel_id=1, source_target_pairs={{0,1},{1,0},{2,3},{3,2},{4,5},{5,4},{6,7},{7,6},{8,9},{9,8},{10,11... | collective-permute-start | bytes 2457608 | tf_op jit(solution)/shard_map/ppermute | solution.py:57
  119.4 18.8 %all-to-all-start.2 = ((bf16[8,64,896]{2,1,0:T(8,128)(2,1)}), bf16[8,64,896]{2,1,0:T(8,128)(2,1)}, u32[]{:S(2)}, u32[]{:S(2)}) async-start(bf16[8,64,896]{2,1,0:T(8,128)(2,1)} %product.3), calls=%async_computation.2 | async-start | bytes 1835008 | tf_op jit(solution)/shard_map/all_to_all | solution.py:137
  150.6 15.6 %collective-permute-start.21 = (bf16[64,5120]{1,0:T(8,128)(2,1)}, bf16[64,5120]{1,0:T(8,128)(2,1)S(1)}, u32[]{:S(2)}, u32[]{:S(2)}) collective-permute-start(bf16[64,5120]{1,0:T(8,128)(2,1)} %attend_slots.1.refs_0_), channel_id=1, source_target_pairs={{0,16},{4,20},{8,24},{12,28},{16,32},{20,36},{24,40},{28,44},{32,4... | collective-permute-start | bytes 1966088 | tf_op jit(solution)/shard_map/ppermute | solution.py:39
  150.6 15.6 %collective-permute-start.22 = (bf16[64,5120]{1,0:T(8,128)(2,1)}, bf16[64,5120]{1,0:T(8,128)(2,1)S(1)}, u32[]{:S(2)}, u32[]{:S(2)}) collective-permute-start(bf16[64,5120]{1,0:T(8,128)(2,1)} %attend_slots.1.refs_0_), channel_id=1, source_target_pairs={{0,48},{4,52},{8,56},{12,60},{16,0},{20,4},{24,8},{28,12},{32,16},... | collective-permute-start | bytes 1966088 | tf_op jit(solution)/shard_map/ppermute | solution.py:39
  153.8 21.8 %collective-permute-start.20 = (bf16[64,5120]{1,0:T(8,128)(2,1)}, bf16[64,5120]{1,0:T(8,128)(2,1)}, u32[]{:S(2)}, u32[]{:S(2)}) collective-permute-start(bf16[64,5120]{1,0:T(8,128)(2,1)} %attend_slots.1.refs_0_), channel_id=1, source_target_pairs={{0,12},{4,8},{8,4},{12,0},{16,28},{20,24},{24,20},{28,16},{32,44},... | collective-permute-start | bytes 1966088 | tf_op jit(solution)/shard_map/ppermute | solution.py:44
  166.1 3.9 %copy-start.6 = (bf16[64,5120]{1,0:T(8,128)(2,1)}, bf16[64,5120]{1,0:T(8,128)(2,1)S(1)}, u32[]{:S(2)}) copy-start(bf16[64,5120]{1,0:T(8,128)(2,1)S(1)} %collective-permute-done.21.refs_1_) | copy-start | bytes 1966084
  166.1 3.9 %copy-start.7 = (bf16[64,5120]{1,0:T(8,128)(2,1)}, bf16[64,5120]{1,0:T(8,128)(2,1)S(1)}, u32[]{:S(2)}) copy-start(bf16[64,5120]{1,0:T(8,128)(2,1)S(1)} %collective-permute-done.22.refs_2_) | copy-start | bytes 1966084
  167.1 12.1 %collective-permute-start.23 = (bf16[64,5120]{1,0:T(8,128)(2,1)}, bf16[64,5120]{1,0:T(8,128)(2,1)}, u32[]{:S(2)}, u32[]{:S(2)}) collective-permute-start(bf16[64,5120]{1,0:T(8,128)(2,1)} %broadcast_select_fusion.2), channel_id=1, source_target_pairs={{0,16},{1,49},{2,18},{3,51},{4,20},{5,53},{6,22},{7,55},{8,24},{9,... | collective-permute-start | bytes 1966088 | tf_op jit(solution)/shard_map/ppermute | solution.py:68
  167.1 24.9 %collective-permute-start.27 = (bf16[320,1280]{1,0:T(8,128)(2,1)}, bf16[320,1280]{1,0:T(8,128)(2,1)S(1)}, u32[]{:S(2)}, u32[]{:S(2)}) collective-permute-start(bf16[320,1280]{1,0:T(8,128)(2,1)} %collective-permute-done.16.refs_10_), channel_id=1, source_target_pairs={{0,1},{1,0},{2,3},{3,2},{4,5},{5,4},{6,7},{7,6},{8,9},{9,8},{10,11... | collective-permute-start | bytes 2457608 | tf_op jit(solution)/shard_map/ppermute | solution.py:57
  170.1 52.1 %collective-permute-start.29 = (bf16[1280,320]{0,1:T(8,128)(2,1)}, bf16[1280,320]{0,1:T(8,128)(2,1)}, u32[]{:S(2)}, u32[]{:S(2)}) collective-permute-start(bf16[1280,320]{0,1:T(8,128)(2,1)} %copy.38), channel_id=1, source_target_pairs={{0,64},{1,65},{2,66},{3,67},{4,68},{5,69},{6,70},{7,71},{8,72},{9,... | collective-permute-start | bytes 2457608 | tf_op jit(solution)/shard_map/ppermute | solution.py:33
  179.3 29.4 %collective-permute-start.24 = (bf16[64,5120]{1,0:T(8,128)(2,1)}, bf16[64,5120]{1,0:T(8,128)(2,1)S(1)}, u32[]{:S(2)}, u32[]{:S(2)}) collective-permute-start(bf16[64,5120]{1,0:T(8,128)(2,1)} %collective-permute-done.20.refs_0_), channel_id=1, source_target_pairs={{0,16},{4,20},{8,24},{12,28},{16,32},{20,36},{24,40},{28,44},{32,4... | collective-permute-start | bytes 1966088 | tf_op jit(solution)/shard_map/ppermute | solution.py:39
  179.3 29.5 %collective-permute-start.25 = (bf16[64,5120]{1,0:T(8,128)(2,1)}, bf16[64,5120]{1,0:T(8,128)(2,1)S(1)}, u32[]{:S(2)}, u32[]{:S(2)}) collective-permute-start(bf16[64,5120]{1,0:T(8,128)(2,1)} %collective-permute-done.20.refs_0_), channel_id=1, source_target_pairs={{0,48},{4,52},{8,56},{12,60},{16,0},{20,4},{24,8},{28,12},{32,16},... | collective-permute-start | bytes 1966088 | tf_op jit(solution)/shard_map/ppermute | solution.py:39
  182.5 26.2 %collective-permute-start.26 = (bf16[64,5120]{1,0:T(8,128)(2,1)}, bf16[64,5120]{1,0:T(8,128)(2,1)}, u32[]{:S(2)}, u32[]{:S(2)}) collective-permute-start(bf16[64,5120]{1,0:T(8,128)(2,1)} %collective-permute-done.23.refs_3_), channel_id=1, source_target_pairs={{0,12},{4,8},{8,4},{12,0},{16,28},{20,24},{24,20},{28,16},{32,44},... | collective-permute-start | bytes 1966088 | tf_op jit(solution)/shard_map/ppermute | solution.py:44
  192.0 8.1 %copy-start.5 = (bf16[320,1280]{1,0:T(8,128)(2,1)}, bf16[320,1280]{1,0:T(8,128)(2,1)S(1)}, u32[]{:S(2)}) copy-start(bf16[320,1280]{1,0:T(8,128)(2,1)S(1)} %collective-permute-done.27.refs_11_) | copy-start | bytes 2457604
  192.0 35.1 %collective-permute-start.28 = (bf16[448,1280]{1,0:T(8,128)(2,1)}, bf16[448,1280]{1,0:T(8,128)(2,1)}, u32[]{:S(2)}, u32[]{:S(2)}) collective-permute-start(bf16[448,1280]{1,0:T(8,128)(2,1)} %fold_part.1), channel_id=1, source_target_pairs={{0,64},{1,65},{2,66},{3,67},{4,68},{5,69},{6,70},{7,71},{8,72},{9,... | collective-permute-start | bytes 3440648 | tf_op jit(solution)/shard_map/ppermute | solution.py:33
  208.7 0.8 copy-start.9
  208.7 1.0 copy-start.10
  218.4 14.2 %all-to-all-start.3 = ((bf16[8,64,640]{2,1,0:T(8,128)(2,1)}), bf16[8,64,640]{2,1,0:T(8,128)(2,1)S(1)}, u32[]{:S(2)}, u32[]{:S(2)}) async-start(bf16[8,64,640]{2,1,0:T(8,128)(2,1)} %product.5), calls=%async_computation.3 | async-start | bytes 1310720 | tf_op jit(solution)/shard_map/all_to_all | solution.py:137
  224.9 2.3 copy-start.8
  233.4 1.1 copy-start.4
where the time goes:
time: 237 us; the launch traced here: 236 us
  waiting for transfers between devices  90.5 us (38%)
  starting transfers between devices  57.2 us (24%)
  Pallas kernels  51.1 us (22%)
  local copies, waits for them, and re-layouts  18.7 us (8%)
  other arithmetic  14 us (6%)
  matrix products  3.02 us (1%)
    ppermute x8, waiting for transfers between devices, along_z(): return lax.ppermute(value, 'shard', pairs)  43.7 us
    pallas_call x3, Pallas kernels, product(): pl.pallas_call(functools.partial(product_kernel, blocks, groups, buffer i...  29.9 us
    all_to_all x2, waiting for transfers between devices, to_owners(): lax.all_to_all(ordered, 'shard', split_axis=0, concat_axis=0, axis_index_...  17.5 us
    ppermute x8, starting transfers between devices, along_z(): return lax.ppermute(value, 'shard', pairs)  13.9 us
    pallas_call x1, Pallas kernels, attend_slots(): pl.pallas_call(attention_kernel, out_shape=jax.ShapeDtypeStruct((rows * S...  12.3 us
    ppermute x2, starting transfers between devices, shifted(): lax.ppermute(value, axis, [(source, source + steps) for source in range(i...  11.9 us
    ppermute x2, waiting for transfers between devices, other_chip(): return lax.ppermute(value, 'rep', [(r, r ^ 2) for r in range(4)])  11.8 us
    ppermute x4, waiting for transfers between devices, mirror_y(): return lax.ppermute(value, 'shard', [(s, s ^ 3) for s in range(count)])  9.29 us
  transfers between devices with their start and end apart: 34, of which 10 were waited for; matrix products, arithmetic and copies ran while one was open for 11% of the time, Pallas kernels for 16%

commit v1 on v0

--- a/solution.py
+++ b/solution.py
@@ -508,17 +508,17 @@
     order = jnp.concatenate([near, far, low_first])
     spread = lax.all_to_all(own_out, "shard", split_axis=0, concat_axis=1, tiled=True)
     turned = rotate_columns(after(spread, same[3]))
-    folded_out = lax.all_to_all(
-        turned, "shard", split_axis=1, concat_axis=0, tiled=True
-    )
     both_bias = jnp.concatenate([own_bias, pair_bias], axis=0)
     part = product(
         same + mirror, qkv_slots[0] + qkv_slots[1], both_bias, after(order, turned)
     )
-    packed = to_owners(after(part, folded_out))
+    packed = to_owners(part)
     out_slots = gather_weights(after(own_out.T, turned), part, packed)
     weights = out_slots[0] + out_slots[1]
-    sent_out = shifted(after(folded_out, part), "role", 1)
+    folded_out = lax.all_to_all(
+        after(turned, part), "shard", split_axis=1, concat_axis=0, tiled=True
+    )
+    sent_out = shifted(folded_out, "role", 1)
     packed = after(packed, out_slots[2], *weights[:6])
     attended = attend_slots(packed, cache_keys[0], cache_values[0], lengths[0], rep_index)
     folded_qkv = rotate_column_part(

time: 237 us -> 235 us (level)
  starting transfers between devices: 57.2 us -> 54.3 us
  waiting for transfers between devices: 90.5 us -> 93.3 us
    all_to_all x1, waiting for transfers between devices: 3.26 us -> 0.01 us  [body(): lax.all_to_all(after(turned, part), 'shard', split_axis=1, concat_axis=0,...]
    all_to_all x0 -> x3, local copies, waits for them, and re-layouts: none -> 3.24 us  [body(): lax.all_to_all(after(turned, part), 'shard', split_axis=1, concat_axis=0,...]
    convert_element_type x2 -> x0, local copies, waits for them, and re-layouts: 3.13 us -> none  [rotate_columns(): (turned.reshape(height, D) * (1.0 / math.sqrt(D))).astype(jnp.bfloat16)]
    ppermute x2, waiting for transfers between devices: 1.21 us -> 3.69 us  [next_y(): return lax.ppermute(value, 'shard', [(s, s ^ 1) for s in range(count)])]
    unnamed x41 -> x42, local copies, waits for them, and re-layouts: 7.05 us -> 6.46 us
  transfers between devices with their start and end apart: 34 -> 34, of which waited for: 10 -> 10; matrix products, arithmetic and copies ran while one was open for 11% -> 11% of each run, Pallas kernels for 16% -> 17%
where the time goes in v1:
time: 235 us; the launch traced here: 234 us
  waiting for transfers between devices  93.3 us (40%)
  starting transfers between devices  54.3 us (23%)
  Pallas kernels  51.5 us (22%)
  local copies, waits for them, and re-layouts  16.9 us (7%)
  other arithmetic  14.3 us (6%)
    ppermute x8, waiting for transfers between devices, along_z(): return lax.ppermute(value, 'shard', pairs)  45.6 us
    pallas_call x3, Pallas kernels, product(): pl.pallas_call(functools.partial(product_kernel, blocks, groups, buffer i...  30.1 us
    all_to_all x2, waiting for transfers between devices, to_owners(): lax.all_to_all(ordered, 'shard', split_axis=0, concat_axis=0, axis_index_...  19.3 us
    ppermute x8, starting transfers between devices, along_z(): return lax.ppermute(value, 'shard', pairs)  14.1 us
    ppermute x2, waiting for transfers between devices, other_chip(): return lax.ppermute(value, 'rep', [(r, r ^ 2) for r in range(4)])  12.7 us
    pallas_call x1, Pallas kernels, attend_slots(): pl.pallas_call(attention_kernel, out_shape=jax.ShapeDtypeStruct((rows * S...  12.5 us
    ppermute x2, starting transfers between devices, shifted(): lax.ppermute(value, axis, [(source, source + steps) for source in range(i...  9.81 us
    ppermute x4, starting transfers between devices, mirror_y(): return lax.ppermute(value, 'shard', [(s, s ^ 3) for s in range(count)])  9.28 us
  transfers between devices with their start and end apart: 34, of which 10 were waited for; matrix products, arithmetic and copies ran while one was open for 11% of the time, Pallas kernels for 17%

profile of v1, /device:TPU:0, one launch (start us, length us, event | category | flops | bytes accessed | tf_op | source)
XLA Modules:
  0.0 233.6 jit_solution(1455978045498794168)
XLA Ops:
  0.7 1.5 reshape.164
  3.1 2.1 collective-permute-start
  5.2 2.2 collective-permute-start.1
  7.4 3.0 %collective-permute-start.3 = (bf16[64,5120]{1,0:T(8,128)(2,1)S(1)}, bf16[64,5120]{1,0:T(8,128)(2,1)}, u32[]{:S(2)}, u32[]{:S(2)}) collective-permute-start(bf16[64,5120]{1,0:T(8,128)(2,1)S(1)} %pad_maximum_fusion.refs_0_), channel_id=1, source_target_pairs={{0,12},{4,8},{8,4},{12,0},{16,28},{20,24},{24,20},{28,16},{32,44},... | collective-permute-start | bytes 1966088 | tf_op jit(solution)/shard_map/ppermute | solution.py:44
  10.4 1.5 collective-permute-start.8
  12.0 10.0 %collective-permute-done.refs_1_ = bf16[64,5120]{1,0:T(8,128)(2,1)S(1)} collective-permute-done((bf16[64,5120]{1,0:T(8,128)(2,1)S(1)}, bf16[64,5120]{1,0:T(8,128)(2,1)S(1)}, u32[]{:S(2)}, u32[]{:S(2)}) %collective-permute-start) | collective-permute-done | bytes 655392 | tf_op jit(solution)/shard_map/ppermute | solution.py:39
  22.1 0.8 copy-done.11
  22.9 0.9 broadcast_select_fusion.3
  23.8 0.5 collective-permute-start.2
  24.3 12.7 %collective-permute-done.8.refs_10_.refs_2_ = bf16[448,1280]{1,0:T(8,128)(2,1)S(1)} collective-permute-done((bf16[448,1280]{1,0:T(8,128)(2,1)}, bf16[448,1280]{1,0:T(8,128)(2,1)S(1)}, u32[]{:S(2)}, u32[]{:S(2)}) %collective-permute-start.8) | collective-permute-done | bytes 1146912 | tf_op jit(solution)/shard_map/ppermute | solution.py:53
  37.1 1.3 collective-permute-done.10.refs_12_
  38.4 2.4 %broadcast_select_fusion = bf16[448,1280]{1,0:T(8,128)(2,1)} fusion(bf16[448,1280]{1,0:T(8,128)(2,1)} %collective-permute-done.10.refs_12_, bf16[448,1280]{1,0:T(8,128)(2,1)S(1)} %collective-permute-done.8.refs_10_.refs_2_, pred[]{:T(512)S(6)} %eq.64), kind=kLoop, calls=%fused_computation.6 | loop fusion | flops 573440 | bytes 3440641 | tf_op jit(solution)/shard_map/jit(_where)/select_n | solution.py:61
  40.8 0.6 collective-permute-start.12
  41.3 1.3 copy.38
  42.7 3.8 %all-to-all-start = ((bf16[16,80,320]{2,1,0:T(8,128)(2,1)}), bf16[16,80,320]{2,1,0:T(8,128)(2,1)S(1)}, u32[]{:S(2)}, u32[]{:S(2)}) async-start(bf16[16,80,320]{2,1,0:T(8,128)(2,1)} %bitcast.3), calls=%async_computation | async-start | bytes 1966080 | tf_op jit(solution)/shard_map/all_to_all | solution.py:509
  46.6 1.9 collective-permute-start.4
  49.4 1.4 collective-permute-start.5
  50.9 20.6 %collective-permute-done.4.refs_5_ = bf16[64,5120]{1,0:T(8,128)(2,1)S(1)} collective-permute-done((bf16[64,5120]{1,0:T(8,128)(2,1)}, bf16[64,5120]{1,0:T(8,128)(2,1)S(1)}, u32[]{:S(2)}, u32[]{:S(2)}) %collective-permute-start.4) | collective-permute-done | bytes 655392 | tf_op jit(solution)/shard_map/ppermute | solution.py:39
  71.4 2.7 %collective-permute-start.6 = (bf16[64,5120]{1,0:T(8,128)(2,1)}, bf16[64,5120]{1,0:T(8,128)(2,1)}, u32[]{:S(2)}, u32[]{:S(2)}) collective-permute-start(bf16[64,5120]{1,0:T(8,128)(2,1)} %collective-permute-done.2.refs_3_), channel_id=1, source_target_pairs={{0,12},{4,8},{8,4},{12,0},{16,28},{20,24},{24,20},{28,16},{32,44},... | collective-permute-start | bytes 1966088 | tf_op jit(solution)/shard_map/ppermute | solution.py:44
  74.5 0.8 all_to_all.37
  75.4 0.6 fusion.5
  76.0 1.5 multiply_convert_fusion
  77.6 1.0 copy.49
  78.6 0.7 collective-permute-start.14
  79.3 8.0 %collective-permute-done.6.refs_7_ = bf16[64,5120]{1,0:T(8,128)(2,1)} collective-permute-done((bf16[64,5120]{1,0:T(8,128)(2,1)}, bf16[64,5120]{1,0:T(8,128)(2,1)}, u32[]{:S(2)}, u32[]{:S(2)}) %collective-permute-start.6) | collective-permute-done | bytes 655392 | tf_op jit(solution)/shard_map/ppermute | solution.py:44
  87.5 0.6 pad_add_fusion.1.order_ref
  88.2 0.6 pad_maximum_fusion.4.refs_16_
  88.9 12.9 %product.3 = bf16[8,64,896]{2,1,0:T(8,128)(2,1)} custom-call(s32[9]{0:T(128)} %pad_add_fusion.1.order_ref, bf16[64,5120]{1,0:T(8,128)(2,1)} %copy-done.10, bf16[64,5120]{1,0:T(8,128)(2,1)} %copy-done.11, bf16[64,5120]{1,0:T(8,128)(2,1)} %collective-permute-done.1.refs_2_, bf16[64,5120]{1,0:T(8,128)(2,1)} %collective-permute-done.2.refs_3_, ...), custom_call_target="tpu_custom_call" | custom-call | flops 4697620480 | bytes 14417920 | tf_op jit(solution)/shard_map/product/pallas_call | solution.py:462
  101.8 2.4 %collective-permute-done.15.refs_8_ = bf16[320,1280]{1,0:T(8,128)(2,1)S(1)} collective-permute-done((bf16[320,1280]{1,0:T(8,128)(2,1)S(1)}, bf16[320,1280]{1,0:T(8,128)(2,1)S(1)}, u32[]{:S(2)}, u32[]{:S(2)}) %collective-permute-start.15) | collective-permute-done | bytes 819232 | tf_op jit(solution)/shard_map/ppermute | solution.py:49
  104.2 1.1 broadcast_select_fusion.1
  105.8 4.4 %all-to-all-start.1 = ((bf16[8,64,896]{2,1,0:T(8,128)(2,1)}), bf16[8,64,896]{2,1,0:T(8,128)(2,1)}, u32[]{:S(2)}, u32[]{:S(2)}) async-start(bf16[8,64,896]{2,1,0:T(8,128)(2,1)} %product.3), calls=%async_computation.1 | async-start | bytes 1835008 | tf_op jit(solution)/shard_map/all_to_all | solution.py:137
  110.6 0.7 pad_maximum_fusion.1
  111.3 14.8 %all-to-all-done.1.packed_ref = bf16[8,64,896]{2,1,0:T(8,128)(2,1)} async-done(((bf16[8,64,896]{2,1,0:T(8,128)(2,1)}), bf16[8,64,896]{2,1,0:T(8,128)(2,1)}, u32[]{:S(2)}, u32[]{:S(2)}) %all-to-all-start.1) | async-done | bytes 917536 | tf_op jit(solution)/shard_map/all_to_all | solution.py:137
  126.1 12.5 %attend_slots.1.refs_0_ = bf16[64,5120]{1,0:T(8,128)(2,1)} custom-call(s32[1]{0:T(128)} %bitcast.1.part_ref, s32[16]{0:T(128)} %bitcast.57, bf16[8,64,896]{2,1,0:T(8,128)(2,1)} %all-to-all-done.1.packed_ref, f32[64,128]{1,0:T(8,128)} %get-tuple-element.56.cosine_ref, f32[64,128]{1,0:T(8,128)} %get-tuple-element.57.sine_ref, bf16[16,128,1024]{2,1,0:T(8,128)(2,1)} %bitcast.49, ...), custom_call_target="tpu_custom_call" | custom-call | flops 2000000000 | bytes 10000000 | tf_op jit(solution)/shard_map/attend_slots/pallas_call | solution.py:354
  138.6 3.2 %collective-permute-start.22 = (bf16[64,5120]{1,0:T(8,128)(2,1)}, bf16[64,5120]{1,0:T(8,128)(2,1)}, u32[]{:S(2)}, u32[]{:S(2)}) collective-permute-start(bf16[64,5120]{1,0:T(8,128)(2,1)} %attend_slots.1.refs_0_), channel_id=1, source_target_pairs={{0,48},{4,52},{8,56},{12,60},{16,0},{20,4},{24,8},{28,12},{32,16},... | collective-permute-start | bytes 1966088 | tf_op jit(solution)/shard_map/ppermute | solution.py:39
  141.9 0.8 all_to_all.40
  142.6 1.2 copy.42
  143.8 3.6 %all-to-all-start.3 = ((bf16[80,16,320]{2,0,1:T(8,128)(2,1)}), bf16[80,16,320]{2,0,1:T(8,128)(2,1)S(1)}, u32[]{:S(2)}, u32[]{:S(2)}) async-start(bf16[80,16,320]{2,0,1:T(8,128)(2,1)} %copy.42), calls=%async_computation.3 | async-start | bytes 1966080 | tf_op jit(solution)/shard_map/all_to_all | solution.py:518
  147.5 3.0 %collective-permute-start.20 = (bf16[64,5120]{1,0:T(8,128)(2,1)}, bf16[64,5120]{1,0:T(8,128)(2,1)}, u32[]{:S(2)}, u32[]{:S(2)}) collective-permute-start(bf16[64,5120]{1,0:T(8,128)(2,1)} %attend_slots.1.refs_0_), channel_id=1, source_target_pairs={{0,12},{4,8},{8,4},{12,0},{16,28},{20,24},{24,20},{28,16},{32,44},... | collective-permute-start | bytes 1966088 | tf_op jit(solution)/shard_map/ppermute | solution.py:44
  150.5 15.0 %collective-permute-done.21.refs_1_ = bf16[64,5120]{1,0:T(8,128)(2,1)S(1)} collective-permute-done((bf16[64,5120]{1,0:T(8,128)(2,1)}, bf16[64,5120]{1,0:T(8,128)(2,1)S(1)}, u32[]{:S(2)}, u32[]{:S(2)}) %collective-permute-start.21) | collective-permute-done | bytes 655392 | tf_op jit(solution)/shard_map/ppermute | solution.py:39
  165.5 1.0 broadcast_select_fusion.2
  167.1 0.7 copy.41.outer_ref
  167.8 0.7 fusion.4.inner_ref
  168.5 1.3 copy.43
  169.8 4.9 %collective-permute-start.29 = (bf16[1280,320]{0,1:T(8,128)(2,1)}, bf16[1280,320]{0,1:T(8,128)(2,1)}, u32[]{:S(2)}, u32[]{:S(2)}) collective-permute-start(bf16[1280,320]{0,1:T(8,128)(2,1)} %copy.43), channel_id=1, source_target_pairs={{0,64},{1,65},{2,66},{3,67},{4,68},{5,69},{6,70},{7,71},{8,72},{9,... | collective-permute-start | bytes 2457608 | tf_op jit(solution)/shard_map/ppermute | solution.py:33
  174.7 4.0 %collective-permute-done.23.refs_3_ = bf16[64,5120]{1,0:T(8,128)(2,1)} collective-permute-done((bf16[64,5120]{1,0:T(8,128)(2,1)}, bf16[64,5120]{1,0:T(8,128)(2,1)}, u32[]{:S(2)}, u32[]{:S(2)}) %collective-permute-start.23) | collective-permute-done | bytes 655392 | tf_op jit(solution)/shard_map/ppermute | solution.py:68
  178.6 3.2 %collective-permute-start.25 = (bf16[64,5120]{1,0:T(8,128)(2,1)}, bf16[64,5120]{1,0:T(8,128)(2,1)}, u32[]{:S(2)}, u32[]{:S(2)}) collective-permute-start(bf16[64,5120]{1,0:T(8,128)(2,1)} %collective-permute-done.20.refs_0_), channel_id=1, source_target_pairs={{0,48},{4,52},{8,56},{12,60},{16,0},{20,4},{24,8},{28,12},{32,16},... | collective-permute-start | bytes 1966088 | tf_op jit(solution)/shard_map/ppermute | solution.py:39
  181.9 0.5 collective-permute-start.26
  182.4 8.9 %fold_part.1 = bf16[448,1280]{1,0:T(8,128)(2,1)} custom-call(f32[40,10]{1,0:T(8,128)} %copy.41.outer_ref, bf16[128,128]{1,0:T(8,128)(2,1)} %fusion.4.inner_ref, bf16[448,1280]{1,0:T(8,128)(2,1)} %bitcast.9.refs_8_.refs_0_, bf16[448,1280]{1,0:T(8,128)(2,1)} %collective-permute-done.7.refs_9_.refs_1_, bf16[448,1280]{1,0:T(8,128)(2,1)} %copy-done.7, ...), custom_call_target="tpu_custom_call" | custom-call | flops 4000000000 | bytes 6000000 | tf_op jit(solution)/shard_map/fold_part/pallas_call | solution.py:208
  191.3 4.9 %collective-permute-start.28 = (bf16[448,1280]{1,0:T(8,128)(2,1)}, bf16[448,1280]{1,0:T(8,128)(2,1)}, u32[]{:S(2)}, u32[]{:S(2)}) collective-permute-start(bf16[448,1280]{1,0:T(8,128)(2,1)} %fold_part.1), channel_id=1, source_target_pairs={{0,64},{1,65},{2,66},{3,67},{4,68},{5,69},{6,70},{7,71},{8,72},{9,... | collective-permute-start | bytes 3440648 | tf_op jit(solution)/shard_map/ppermute | solution.py:33
  196.2 0.7 pad_add_fusion.2.order_ref
  196.8 0.7 pad_add_fusion.order_ref
  197.5 0.6 broadcast_in_dim.30.refs_12_
  198.1 8.6 %product.4.refs_13_ = bf16[8,64,640]{2,1,0:T(8,128)(2,1)} custom-call(s32[5]{0:T(128)} %pad_add_fusion.2.order_ref, bf16[64,5120]{1,0:T(8,128)(2,1)} %attend_slots.1.refs_0_, bf16[64,5120]{1,0:T(8,128)(2,1)} %copy-done.6, bf16[64,5120]{1,0:T(8,128)(2,1)} %collective-permute-done.22.refs_2_, bf16[64,5120]{1,0:T(8,128)(2,1)} %collective-permute-done.23.refs_3_, ...), custom_call_target="tpu_custom_call" | custom-call | flops 1677721600 | bytes 9175040 | tf_op jit(solution)/shard_map/product/pallas_call | solution.py:462
  206.8 0.8 copy-done.9
  207.6 8.6 %product.5 = bf16[8,64,640]{2,1,0:T(8,128)(2,1)} custom-call(s32[5]{0:T(128)} %pad_add_fusion.order_ref, bf16[64,5120]{1,0:T(8,128)(2,1)} %collective-permute-done.20.refs_0_, bf16[64,5120]{1,0:T(8,128)(2,1)} %copy-done.9, bf16[64,5120]{1,0:T(8,128)(2,1)} %collective-permute-done.25.refs_2_, ...), custom_call_target="tpu_custom_call", output_to_operand_aliasing={{}: (14, {})} | custom-call | flops 1677721600 | bytes 9175040 | tf_op jit(solution)/shard_map/product/pallas_call | solution.py:462
  216.2 4.3 %all-to-all-start.2 = ((bf16[8,64,640]{2,1,0:T(8,128)(2,1)}), bf16[8,64,640]{2,1,0:T(8,128)(2,1)S(1)}, u32[]{:S(2)}, u32[]{:S(2)}) async-start(bf16[8,64,640]{2,1,0:T(8,128)(2,1)} %product.5), calls=%async_computation.2 | async-start | bytes 1310720 | tf_op jit(solution)/shard_map/all_to_all | solution.py:137
  220.4 1.6 copy.44
  222.0 1.2 select_bitcast_fusion.1
  223.2 2.3 copy.45
  225.4 1.1 select_bitcast_fusion
  226.6 4.5 %all-to-all-done.2 = bf16[8,64,640]{2,1,0:T(8,128)(2,1)S(1)} async-done(((bf16[8,64,640]{2,1,0:T(8,128)(2,1)}), bf16[8,64,640]{2,1,0:T(8,128)(2,1)S(1)}, u32[]{:S(2)}, u32[]{:S(2)}) %all-to-all-start.2) | async-done | bytes 655392 | tf_op jit(solution)/shard_map/all_to_all | solution.py:137
  231.1 0.8 copy.40
  232.4 1.2 add_convert_fusion
  (104 shorter events, 4.9 us)
Async XLA Ops:
  0.6 1.5 copy-start.3
  0.7 2.0 copy-start.13
  3.1 37.7 %copy-start.10 = (bf16[64,5120]{1,0:T(8,128)(2,1)}, bf16[64,5120]{1,0:T(8,128)(2,1)S(1)}, u32[]{:S(2)}) copy-start(bf16[64,5120]{1,0:T(8,128)(2,1)S(1)} %pad_maximum_fusion.refs_0_) | copy-start | bytes 1966084
  3.1 18.9 %collective-permute-start = (bf16[64,5120]{1,0:T(8,128)(2,1)S(1)}, bf16[64,5120]{1,0:T(8,128)(2,1)S(1)}, u32[]{:S(2)}, u32[]{:S(2)}) collective-permute-start(bf16[64,5120]{1,0:T(8,128)(2,1)S(1)} %pad_maximum_fusion.refs_0_), channel_id=1, source_target_pairs={{0,16},{4,20},{8,24},{12,28},{16,32},{20,36},{24,40},{28,44},{32,4... | collective-permute-start | bytes 1966088 | tf_op jit(solution)/shard_map/ppermute | solution.py:39
  5.2 16.9 %collective-permute-start.1 = (bf16[64,5120]{1,0:T(8,128)(2,1)S(1)}, bf16[64,5120]{1,0:T(8,128)(2,1)}, u32[]{:S(2)}, u32[]{:S(2)}) collective-permute-start(bf16[64,5120]{1,0:T(8,128)(2,1)S(1)} %pad_maximum_fusion.refs_0_), channel_id=1, source_target_pairs={{0,48},{4,52},{8,56},{12,60},{16,0},{20,4},{24,8},{28,12},{32,16},... | collective-permute-start | bytes 1966088 | tf_op jit(solution)/shard_map/ppermute | solution.py:39
  7.4 39.2 %collective-permute-start.3 = (bf16[64,5120]{1,0:T(8,128)(2,1)S(1)}, bf16[64,5120]{1,0:T(8,128)(2,1)}, u32[]{:S(2)}, u32[]{:S(2)}) collective-permute-start(bf16[64,5120]{1,0:T(8,128)(2,1)S(1)} %pad_maximum_fusion.refs_0_), channel_id=1, source_target_pairs={{0,12},{4,8},{8,4},{12,0},{16,28},{20,24},{24,20},{28,16},{32,44},... | collective-permute-start | bytes 1966088 | tf_op jit(solution)/shard_map/ppermute | solution.py:44
  10.4 26.7 %collective-permute-start.8 = (bf16[448,1280]{1,0:T(8,128)(2,1)}, bf16[448,1280]{1,0:T(8,128)(2,1)S(1)}, u32[]{:S(2)}, u32[]{:S(2)}) collective-permute-start(bf16[448,1280]{1,0:T(8,128)(2,1)} %bitcast.9.refs_8_.refs_0_), channel_id=1, source_target_pairs={{0,2},{1,3},{2,0},{3,1},{4,6},{5,7},{6,4},{7,5},{8,10},{9,11},{10,... | collective-permute-start | bytes 3440648 | tf_op jit(solution)/shard_map/ppermute | solution.py:53
  11.9 26.5 %collective-permute-start.10 = (bf16[448,1280]{1,0:T(8,128)(2,1)}, bf16[448,1280]{1,0:T(8,128)(2,1)}, u32[]{:S(2)}, u32[]{:S(2)}) collective-permute-start(bf16[448,1280]{1,0:T(8,128)(2,1)} %bitcast.9.refs_8_.refs_0_), channel_id=1, source_target_pairs={{0,4},{4,0},{8,12},{12,8},{16,20},{20,16},{24,28},{28,24},{32,36},... | collective-permute-start | bytes 3440648 | tf_op jit(solution)/shard_map/ppermute | solution.py:49
  22.0 0.8 copy-start.11
  22.0 27.4 %collective-permute-start.7 = (bf16[448,1280]{1,0:T(8,128)(2,1)}, bf16[448,1280]{1,0:T(8,128)(2,1)}, u32[]{:S(2)}, u32[]{:S(2)}) collective-permute-start(bf16[448,1280]{1,0:T(8,128)(2,1)} %bitcast.9.refs_8_.refs_0_), channel_id=1, source_target_pairs={{0,1},{1,0},{2,3},{3,2},{4,5},{5,4},{6,7},{7,6},{8,9},{9,8},{10,11... | collective-permute-start | bytes 3440648 | tf_op jit(solution)/shard_map/ppermute | solution.py:57
  23.8 17.6 %copy-start = (bf16[1,1280,320]{1,2,0:T(8,128)(2,1)S(1)}, bf16[1,1280,320]{1,2,0:T(8,128)(2,1)}, u32[]{:S(2)}) copy-start(bf16[1,1280,320]{1,2,0:T(8,128)(2,1)} %param.13) | copy-start | bytes 2457604
  23.8 22.8 %collective-permute-start.2 = (bf16[64,5120]{1,0:T(8,128)(2,1)}, bf16[64,5120]{1,0:T(8,128)(2,1)}, u32[]{:S(2)}, u32[]{:S(2)}) collective-permute-start(bf16[64,5120]{1,0:T(8,128)(2,1)} %broadcast_select_fusion.3), channel_id=1, source_target_pairs={{0,16},{1,49},{2,18},{3,51},{4,20},{5,53},{6,22},{7,55},{8,24},{9,... | collective-permute-start | bytes 1966088 | tf_op jit(solution)/shard_map/ppermute | solution.py:68
  37.1 3.7 %copy-start.7 = (bf16[448,1280]{1,0:T(8,128)(2,1)}, bf16[448,1280]{1,0:T(8,128)(2,1)S(1)}, u32[]{:S(2)}) copy-start(bf16[448,1280]{1,0:T(8,128)(2,1)S(1)} %collective-permute-done.8.refs_10_.refs_2_) | copy-start | bytes 3440644
  40.8 33.4 %collective-permute-start.12 = (bf16[448,1280]{1,0:T(8,128)(2,1)}, bf16[448,1280]{1,0:T(8,128)(2,1)}, u32[]{:S(2)}, u32[]{:S(2)}) collective-permute-start(bf16[448,1280]{1,0:T(8,128)(2,1)} %broadcast_select_fusion), channel_id=1, source_target_pairs={{0,2},{1,5},{2,0},{3,7},{4,6},{5,1},{6,4},{7,3},{8,10},{9,13},{10,... | collective-permute-start | bytes 3440648 | tf_op jit(solution)/shard_map/ppermute | solution.py:68
  42.7 5.9 %copy-start.17 = (f32[1,20]{1,0:T(1,128)S(1)}, f32[1,20]{1,0:T(1,128)}, u32[]{:S(2)}) copy-start(f32[1,20]{1,0:T(1,128)} %constant.189.clone.1) | copy-start | bytes 244
  42.7 6.1 %copy-start.15 = (f32[2,2]{0,1:T(2,128)S(1)}, f32[2,2]{0,1:T(2,128)}, u32[]{:S(2)}) copy-start(f32[2,2]{0,1:T(2,128)} %constant.213.clone) | copy-start | bytes 52
  42.7 31.4 %copy-start.16 = (s32[4]{0:T(128)S(1)}, s32[4]{0:T(128)}, u32[]{:S(2)}) copy-start(s32[4]{0:T(128)} %constant.212.clone) | copy-start | bytes 52
  42.7 31.6 %all-to-all-start = ((bf16[16,80,320]{2,1,0:T(8,128)(2,1)}), bf16[16,80,320]{2,1,0:T(8,128)(2,1)S(1)}, u32[]{:S(2)}, u32[]{:S(2)}) async-start(bf16[16,80,320]{2,1,0:T(8,128)(2,1)} %bitcast.3), calls=%async_computation | async-start | bytes 1966080 | tf_op jit(solution)/shard_map/all_to_all | solution.py:509
  46.6 24.9 %collective-permute-start.4 = (bf16[64,5120]{1,0:T(8,128)(2,1)}, bf16[64,5120]{1,0:T(8,128)(2,1)S(1)}, u32[]{:S(2)}, u32[]{:S(2)}) collective-permute-start(bf16[64,5120]{1,0:T(8,128)(2,1)} %collective-permute-done.3.refs_4_), channel_id=1, source_target_pairs={{0,16},{4,20},{8,24},{12,28},{16,32},{20,36},{24,40},{28,44},{32,4... | collective-permute-start | bytes 1966088 | tf_op jit(solution)/shard_map/ppermute | solution.py:39
  48.8 40.0 %collective-permute-start.9 = (bf16[448,1280]{1,0:T(8,128)(2,1)}, bf16[448,1280]{1,0:T(8,128)(2,1)}, u32[]{:S(2)}, u32[]{:S(2)}) collective-permute-start(bf16[448,1280]{1,0:T(8,128)(2,1)} %copy-done.7), channel_id=1, source_target_pairs={{0,1},{1,0},{2,3},{3,2},{4,5},{5,4},{6,7},{7,6},{8,9},{9,8},{10,11... | collective-permute-start | bytes 3440648 | tf_op jit(solution)/shard_map/ppermute | solution.py:57
  48.9 39.9 %collective-permute-start.11 = (bf16[448,1280]{1,0:T(8,128)(2,1)}, bf16[448,1280]{1,0:T(8,128)(2,1)}, u32[]{:S(2)}, u32[]{:S(2)}) collective-permute-start(bf16[448,1280]{1,0:T(8,128)(2,1)} %collective-permute-done.10.refs_12_), channel_id=1, source_target_pairs={{0,1},{1,0},{2,3},{3,2},{4,5},{5,4},{6,7},{7,6},{8,9},{9,8},{10,11... | collective-permute-start | bytes 3440648 | tf_op jit(solution)/shard_map/ppermute | solution.py:57
  49.4 29.2 %collective-permute-start.5 = (bf16[64,5120]{1,0:T(8,128)(2,1)}, bf16[64,5120]{1,0:T(8,128)(2,1)}, u32[]{:S(2)}, u32[]{:S(2)}) collective-permute-start(bf16[64,5120]{1,0:T(8,128)(2,1)} %collective-permute-done.3.refs_4_), channel_id=1, source_target_pairs={{0,48},{4,52},{8,56},{12,60},{16,0},{20,4},{24,8},{28,12},{32,16},... | collective-permute-start | bytes 1966088 | tf_op jit(solution)/shard_map/ppermute | solution.py:39
  71.4 2.8 %copy-start.18 = (bf16[64,5120]{1,0:T(8,128)(2,1)}, bf16[64,5120]{1,0:T(8,128)(2,1)S(1)}, u32[]{:S(2)}) copy-start(bf16[64,5120]{1,0:T(8,128)(2,1)S(1)} %collective-permute-done.4.refs_5_) | copy-start | bytes 1966084
  71.4 15.8 %collective-permute-start.6 = (bf16[64,5120]{1,0:T(8,128)(2,1)}, bf16[64,5120]{1,0:T(8,128)(2,1)}, u32[]{:S(2)}, u32[]{:S(2)}) collective-permute-start(bf16[64,5120]{1,0:T(8,128)(2,1)} %collective-permute-done.2.refs_3_), channel_id=1, source_target_pairs={{0,12},{4,8},{8,4},{12,0},{16,28},{20,24},{24,20},{28,16},{32,44},... | collective-permute-start | bytes 1966088 | tf_op jit(solution)/shard_map/ppermute | solution.py:44
  74.1 14.7 %collective-permute-start.13 = (bf16[448,1280]{1,0:T(8,128)(2,1)}, bf16[448,1280]{1,0:T(8,128)(2,1)}, u32[]{:S(2)}, u32[]{:S(2)}) collective-permute-start(bf16[448,1280]{1,0:T(8,128)(2,1)} %collective-permute-done.12.refs_14_), channel_id=1, source_target_pairs={{0,1},{1,0},{2,3},{3,2},{4,5},{5,4},{6,7},{7,6},{8,9},{9,8},{10,11... | collective-permute-start | bytes 3440648 | tf_op jit(solution)/shard_map/ppermute | solution.py:57
  77.6 9.9 %copy-start.12 = (bf16[1,7168]{1,0:T(2,128)(2,1)S(1)}, bf16[1,7168]{1,0:T(2,128)(2,1)}, u32[]{:S(2)}) copy-start(bf16[1,7168]{1,0:T(2,128)(2,1)} %param.12) | copy-start | bytes 43012
  78.6 23.2 %collective-permute-start.14 = (bf16[320,1280]{1,0:T(8,128)(2,1)S(1)}, bf16[320,1280]{1,0:T(8,128)(2,1)S(1)}, u32[]{:S(2)}, u32[]{:S(2)}) collective-permute-start(bf16[320,1280]{1,0:T(8,128)(2,1)S(1)} %bitcast.46), channel_id=1, source_target_pairs={{0,2},{1,3},{2,0},{3,1},{4,6},{5,7},{6,4},{7,5},{8,10},{9,11},{10,... | collective-permute-start | bytes 2457608 | tf_op jit(solution)/shard_map/ppermute | solution.py:53
  87.2 16.9 %collective-permute-start.15 = (bf16[320,1280]{1,0:T(8,128)(2,1)S(1)}, bf16[320,1280]{1,0:T(8,128)(2,1)S(1)}, u32[]{:S(2)}, u32[]{:S(2)}) collective-permute-start(bf16[320,1280]{1,0:T(8,128)(2,1)S(1)} %bitcast.47), channel_id=1, source_target_pairs={{0,4},{4,0},{8,12},{12,8},{16,20},{20,16},{24,28},{28,24},{32,36},... | collective-permute-start | bytes 2457608 | tf_op jit(solution)/shard_map/ppermute | solution.py:49
  88.8 22.5 %collective-permute-start.17 = (bf16[320,1280]{1,0:T(8,128)(2,1)S(1)}, bf16[320,1280]{1,0:T(8,128)(2,1)}, u32[]{:S(2)}, u32[]{:S(2)}) collective-permute-start(bf16[320,1280]{1,0:T(8,128)(2,1)S(1)} %bitcast.48), channel_id=1, source_target_pairs={{0,1},{1,0},{2,3},{3,2},{4,5},{5,4},{6,7},{7,6},{8,9},{9,8},{10,11... | collective-permute-start | bytes 2457608 | tf_op jit(solution)/shard_map/ppermute | solution.py:57
  101.8 4.0 %copy-start.1 = (bf16[320,1280]{1,0:T(8,128)(2,1)}, bf16[320,1280]{1,0:T(8,128)(2,1)S(1)}, u32[]{:S(2)}) copy-start(bf16[320,1280]{1,0:T(8,128)(2,1)S(1)} %collective-permute-done.14.refs_6_) | copy-start | bytes 2457604
  104.2 1.6 copy-start.2
  105.3 4.9 %copy-start.14 = (s32[1,16]{1,0:T(1,128)S(1)}, s32[1,16]{1,0:T(1,128)}, u32[]{:S(2)}) copy-start(s32[1,16]{1,0:T(1,128)} %param.18) | copy-start | bytes 196
  105.3 20.9 %collective-permute-start.16 = (bf16[320,1280]{1,0:T(8,128)(2,1)}, bf16[320,1280]{1,0:T(8,128)(2,1)}, u32[]{:S(2)}, u32[]{:S(2)}) collective-permute-start(bf16[320,1280]{1,0:T(8,128)(2,1)} %broadcast_select_fusion.1), channel_id=1, source_target_pairs={{0,2},{1,5},{2,0},{3,7},{4,6},{5,1},{6,4},{7,3},{8,10},{9,13},{10,... | collective-permute-start | bytes 2457608 | tf_op jit(solution)/shard_map/ppermute | solution.py:68
  105.3 20.9 %collective-permute-start.18 = (bf16[320,1280]{1,0:T(8,128)(2,1)S(1)}, bf16[320,1280]{1,0:T(8,128)(2,1)}, u32[]{:S(2)}, u32[]{:S(2)}) collective-permute-start(bf16[320,1280]{1,0:T(8,128)(2,1)S(1)} %collective-permute-done.14.refs_6_), channel_id=1, source_target_pairs={{0,1},{1,0},{2,3},{3,2},{4,5},{5,4},{6,7},{7,6},{8,9},{9,8},{10,11... | collective-permute-start | bytes 2457608 | tf_op jit(solution)/shard_map/ppermute | solution.py:57
  105.3 20.9 %collective-permute-start.19 = (bf16[320,1280]{1,0:T(8,128)(2,1)S(1)}, bf16[320,1280]{1,0:T(8,128)(2,1)}, u32[]{:S(2)}, u32[]{:S(2)}) collective-permute-start(bf16[320,1280]{1,0:T(8,128)(2,1)S(1)} %collective-permute-done.15.refs_8_), channel_id=1, source_target_pairs={{0,1},{1,0},{2,3},{3,2},{4,5},{5,4},{6,7},{7,6},{8,9},{9,8},{10,11... | collective-permute-start | bytes 2457608 | tf_op jit(solution)/shard_map/ppermute | solution.py:57
  105.8 20.3 %all-to-all-start.1 = ((bf16[8,64,896]{2,1,0:T(8,128)(2,1)}), bf16[8,64,896]{2,1,0:T(8,128)(2,1)}, u32[]{:S(2)}, u32[]{:S(2)}) async-start(bf16[8,64,896]{2,1,0:T(8,128)(2,1)} %product.3), calls=%async_computation.1 | async-start | bytes 1835008 | tf_op jit(solution)/shard_map/all_to_all | solution.py:137
  126.1 15.7 %copy-start.5 = (bf16[10,8,40,128]{3,1,2,0:T(8,128)(2,1)S(1)}, bf16[10,8,40,128]{3,1,2,0:T(8,128)(2,1)}, u32[]{:S(2)}) copy-start(bf16[10,8,40,128]{3,1,2,0:T(8,128)(2,1)} %copy.49) | copy-start | bytes 2457604
  138.6 26.9 %collective-permute-start.21 = (bf16[64,5120]{1,0:T(8,128)(2,1)}, bf16[64,5120]{1,0:T(8,128)(2,1)S(1)}, u32[]{:S(2)}, u32[]{:S(2)}) collective-permute-start(bf16[64,5120]{1,0:T(8,128)(2,1)} %attend_slots.1.refs_0_), channel_id=1, source_target_pairs={{0,16},{4,20},{8,24},{12,28},{16,32},{20,36},{24,40},{28,44},{32,4... | collective-permute-start | bytes 1966088 | tf_op jit(solution)/shard_map/ppermute | solution.py:39
  138.6 26.9 %collective-permute-start.22 = (bf16[64,5120]{1,0:T(8,128)(2,1)}, bf16[64,5120]{1,0:T(8,128)(2,1)}, u32[]{:S(2)}, u32[]{:S(2)}) collective-permute-start(bf16[64,5120]{1,0:T(8,128)(2,1)} %attend_slots.1.refs_0_), channel_id=1, source_target_pairs={{0,48},{4,52},{8,56},{12,60},{16,0},{20,4},{24,8},{28,12},{32,16},... | collective-permute-start | bytes 1966088 | tf_op jit(solution)/shard_map/ppermute | solution.py:39
  143.8 24.6 %all-to-all-start.3 = ((bf16[80,16,320]{2,0,1:T(8,128)(2,1)}), bf16[80,16,320]{2,0,1:T(8,128)(2,1)S(1)}, u32[]{:S(2)}, u32[]{:S(2)}) async-start(bf16[80,16,320]{2,0,1:T(8,128)(2,1)} %copy.42), calls=%async_computation.3 | async-start | bytes 1966080 | tf_op jit(solution)/shard_map/all_to_all | solution.py:518
  147.5 27.2 %collective-permute-start.20 = (bf16[64,5120]{1,0:T(8,128)(2,1)}, bf16[64,5120]{1,0:T(8,128)(2,1)}, u32[]{:S(2)}, u32[]{:S(2)}) collective-permute-start(bf16[64,5120]{1,0:T(8,128)(2,1)} %attend_slots.1.refs_0_), channel_id=1, source_target_pairs={{0,12},{4,8},{8,4},{12,0},{16,28},{20,24},{24,20},{28,16},{32,44},... | collective-permute-start | bytes 1966088 | tf_op jit(solution)/shard_map/ppermute | solution.py:44
  165.5 4.2 %copy-start.6 = (bf16[64,5120]{1,0:T(8,128)(2,1)}, bf16[64,5120]{1,0:T(8,128)(2,1)S(1)}, u32[]{:S(2)}) copy-start(bf16[64,5120]{1,0:T(8,128)(2,1)S(1)} %collective-permute-done.21.refs_1_) | copy-start | bytes 1966084
  166.5 12.1 %collective-permute-start.23 = (bf16[64,5120]{1,0:T(8,128)(2,1)}, bf16[64,5120]{1,0:T(8,128)(2,1)}, u32[]{:S(2)}, u32[]{:S(2)}) collective-permute-start(bf16[64,5120]{1,0:T(8,128)(2,1)} %broadcast_select_fusion.2), channel_id=1, source_target_pairs={{0,16},{1,49},{2,18},{3,51},{4,20},{5,53},{6,22},{7,55},{8,24},{9,... | collective-permute-start | bytes 1966088 | tf_op jit(solution)/shard_map/ppermute | solution.py:68
  166.5 24.8 %collective-permute-start.27 = (bf16[320,1280]{1,0:T(8,128)(2,1)}, bf16[320,1280]{1,0:T(8,128)(2,1)S(1)}, u32[]{:S(2)}, u32[]{:S(2)}) collective-permute-start(bf16[320,1280]{1,0:T(8,128)(2,1)} %collective-permute-done.16.refs_10_), channel_id=1, source_target_pairs={{0,1},{1,0},{2,3},{3,2},{4,5},{5,4},{6,7},{7,6},{8,9},{9,8},{10,11... | collective-permute-start | bytes 2457608 | tf_op jit(solution)/shard_map/ppermute | solution.py:57
  169.8 50.7 %collective-permute-start.29 = (bf16[1280,320]{0,1:T(8,128)(2,1)}, bf16[1280,320]{0,1:T(8,128)(2,1)}, u32[]{:S(2)}, u32[]{:S(2)}) collective-permute-start(bf16[1280,320]{0,1:T(8,128)(2,1)} %copy.43), channel_id=1, source_target_pairs={{0,64},{1,65},{2,66},{3,67},{4,68},{5,69},{6,70},{7,71},{8,72},{9,... | collective-permute-start | bytes 2457608 | tf_op jit(solution)/shard_map/ppermute | solution.py:33
  178.6 28.1 %collective-permute-start.24 = (bf16[64,5120]{1,0:T(8,128)(2,1)}, bf16[64,5120]{1,0:T(8,128)(2,1)S(1)}, u32[]{:S(2)}, u32[]{:S(2)}) collective-permute-start(bf16[64,5120]{1,0:T(8,128)(2,1)} %collective-permute-done.20.refs_0_), channel_id=1, source_target_pairs={{0,16},{4,20},{8,24},{12,28},{16,32},{20,36},{24,40},{28,44},{32,4... | collective-permute-start | bytes 1966088 | tf_op jit(solution)/shard_map/ppermute | solution.py:39
  178.6 28.1 %collective-permute-start.25 = (bf16[64,5120]{1,0:T(8,128)(2,1)}, bf16[64,5120]{1,0:T(8,128)(2,1)}, u32[]{:S(2)}, u32[]{:S(2)}) collective-permute-start(bf16[64,5120]{1,0:T(8,128)(2,1)} %collective-permute-done.20.refs_0_), channel_id=1, source_target_pairs={{0,48},{4,52},{8,56},{12,60},{16,0},{20,4},{24,8},{28,12},{32,16},... | collective-permute-start | bytes 1966088 | tf_op jit(solution)/shard_map/ppermute | solution.py:39
  181.9 24.9 %collective-permute-start.26 = (bf16[64,5120]{1,0:T(8,128)(2,1)}, bf16[64,5120]{1,0:T(8,128)(2,1)}, u32[]{:S(2)}, u32[]{:S(2)}) collective-permute-start(bf16[64,5120]{1,0:T(8,128)(2,1)} %collective-permute-done.23.refs_3_), channel_id=1, source_target_pairs={{0,12},{4,8},{8,4},{12,0},{16,28},{20,24},{24,20},{28,16},{32,44},... | collective-permute-start | bytes 1966088 | tf_op jit(solution)/shard_map/ppermute | solution.py:44
  191.3 6.8 %copy-start.4 = (bf16[320,1280]{1,0:T(8,128)(2,1)}, bf16[320,1280]{1,0:T(8,128)(2,1)S(1)}, u32[]{:S(2)}) copy-start(bf16[320,1280]{1,0:T(8,128)(2,1)S(1)} %collective-permute-done.27.refs_11_) | copy-start | bytes 2457604
  191.3 34.2 %collective-permute-start.28 = (bf16[448,1280]{1,0:T(8,128)(2,1)}, bf16[448,1280]{1,0:T(8,128)(2,1)}, u32[]{:S(2)}, u32[]{:S(2)}) collective-permute-start(bf16[448,1280]{1,0:T(8,128)(2,1)} %fold_part.1), channel_id=1, source_target_pairs={{0,64},{1,65},{2,66},{3,67},{4,68},{5,69},{6,70},{7,71},{8,72},{9,... | collective-permute-start | bytes 3440648 | tf_op jit(solution)/shard_map/ppermute | solution.py:33
  206.7 0.8 copy-start.9
  216.2 14.9 %all-to-all-start.2 = ((bf16[8,64,640]{2,1,0:T(8,128)(2,1)}), bf16[8,64,640]{2,1,0:T(8,128)(2,1)S(1)}, u32[]{:S(2)}, u32[]{:S(2)}) async-start(bf16[8,64,640]{2,1,0:T(8,128)(2,1)} %product.5), calls=%async_computation.2 | async-start | bytes 1310720 | tf_op jit(solution)/shard_map/all_to_all | solution.py:137
  223.2 2.3 copy-start.8
